TPU v7x, 512 devices: a whole 4x4x16 slice. The times are simulated.
512 devices in a mesh: slab: 32 (over x, y, core), pencil: 16 (over z).
Axes of the slice: x: 4, y: 4, z: 16, core: 2. Of those that a mesh axis runs over, the one named last changes fastest.
Arguments:
- orbitals: float32 [4, 192, 192, 192], P(None, 'slab', 'pencil'), may hold values from -6 to 6
- potential: float32 [192, 192, 192], P('slab', 'pencil'), may hold values from 0.5 to 2.5
- unlocked: int32 [4], replicated, may hold values 0 or 1
Outputs:
- orthonormal: float32 [4, 192, 192, 192], P(None, 'slab', 'pencil')
Inputs may be any that keep to these rules, and one draw needn't show every extreme that they name: `unlocked`: 1 marks a band that is filtered, 0 a locked band kept as it is.
All inputs are finite; a program needn't handle non-finite values.
Results may differ from a plain program's by a relative error of at most 0.00005.
Values sent between devices are 32-bit elements; how exact they have to be, the bound alone decides.
No kernel may reach another device: no remote copies, remote signals or barrier semaphores. Data moves between devices by JAX's collectives and lax.ppermute only.
A program may use at most 64 MiB of HBM per device.

v0:
```python
import math

import jax
import jax.numpy as jnp
from jax import lax
from jax.sharding import PartitionSpec as P

NG = 192


kinetic_scale = 4.0
filter_center = 1.0
filter_half = 1.5
highest = lax.Precision.HIGHEST


def frequencies(number, length):
    index = jnp.arange(number, dtype=jnp.int32)
    return jnp.where(index < length // 2, index, index - length)


def tables(number, length):
    modes = frequencies(number, length)
    places = jnp.arange(length, dtype=jnp.int32)
    product = places[:, None] * modes[None, :] % length
    angle = 2.0 * math.pi / length * product.astype(jnp.float32)
    return (jnp.cos(angle), jnp.sin(angle))


def forward_table(cosine, sine):
    return jnp.stack([jnp.stack([cosine, -sine], 1), jnp.stack([sine, cosine], 1)], 1)


def inverse_table(cosine, sine):
    cos_t = cosine.T
    sin_t = sine.T
    return jnp.stack([jnp.stack([cos_t, sin_t], 1), jnp.stack([-sin_t, cos_t], 1)], 1)


def local(orbitals, potential, unlocked):
    length = orbitals.shape[3]
    cos_k, sin_k = tables(length, length)
    cos_f, sin_f = tables(length, length)
    first_forward = jnp.stack([cos_k, -sin_k], 1)
    first_inverse = jnp.stack([cos_k.T, -sin_k.T], 1)
    second_forward = forward_table(cos_k, sin_k)
    second_inverse = inverse_table(cos_k, sin_k)
    depth_forward = forward_table(cos_f, sin_f)
    depth_inverse = inverse_table(cos_f, sin_f)
    pencil_block = length // lax.axis_size("pencil")
    slab_block = length // lax.axis_size("slab")
    kept_list = frequencies(length, length)
    third_modes = lax.dynamic_slice_in_dim(
        kept_list, lax.axis_index("pencil") * pencil_block, pencil_block
    ).astype(jnp.float32)
    second_modes = lax.dynamic_slice_in_dim(
        kept_list, lax.axis_index("slab") * slab_block, slab_block
    ).astype(jnp.float32)
    first_modes = frequencies(length, length).astype(jnp.float32)
    squared = (
        third_modes[:, None, None] ** 2
        + second_modes[None, :, None] ** 2
        + first_modes[None, None, :] ** 2
    )
    radius = float((length // 4) ** 2)
    kinetic = jnp.where(squared < radius, kinetic_scale * squared / radius, 0.0)
    lines_k = jnp.einsum("bacx,xrk->bacrk", orbitals, first_forward, precision=highest)
    along_f = jnp.einsum(
        "bacrk,crsf->baksf",
        lax.all_to_all(lines_k, "pencil", split_axis=4, concat_axis=2, tiled=True),
        second_forward,
        precision=highest,
    )
    spectra = jnp.einsum(
        "baksf,astg->bkftg",
        lax.all_to_all(along_f, "slab", split_axis=4, concat_axis=1, tiled=True),
        depth_forward,
        precision=highest,
    )
    spectra = spectra * kinetic[None, :, :, None, :]
    along_a = jnp.einsum("bkftg,gtsa->bkfsa", spectra, depth_inverse, precision=highest)
    returned = lax.all_to_all(along_a, "slab", split_axis=4, concat_axis=2, tiled=True)
    rows_c = jnp.einsum("bkfsa,fsrc->bkarc", returned, second_inverse, precision=highest)
    lines_x = lax.all_to_all(rows_c, "pencil", split_axis=4, concat_axis=1, tiled=True)
    kinetic_part = jnp.einsum("bkarc,krx->bacx", lines_x, first_inverse, precision=highest)
    kinetic_part = kinetic_part / float(NG**3)
    applied = kinetic_part + potential[None] * orbitals
    filtered = jnp.where(
        unlocked[:, None, None, None] == 1,
        (applied - filter_center * orbitals) / filter_half,
        orbitals,
    )
    number = filtered.shape[0]
    flattened = filtered.reshape(number, -1)
    partial_intersection = jnp.dot(flattened, flattened.T, precision=highest) / float(NG**3)
    intersection = lax.psum(partial_intersection, ("slab", "pencil"))
    factor = jnp.linalg.cholesky(intersection)
    result = jax.scipy.linalg.solve_triangular(factor, flattened, lower=True)
    return result.reshape(filtered.shape)


def solution(mesh):
    in_specs = (P(None, "slab", "pencil", None), P("slab", "pencil", None), P())
    out_specs = P(None, "slab", "pencil", None)
    return jax.shard_map(local, mesh=mesh, in_specs=in_specs, out_specs=out_specs, check_vma=False)
```

profile of v0, /device:TPU:1, one launch (start us, length us, event | category | flops | bytes accessed | tf_op | source)
XLA Modules:
  0.0 365.7 jit_solution(14531609065697997235)
XLA Ops:
  0.0 1.7 fusion.28
  1.7 1.8 convolution_bitcast_fusion.4
  3.5 3.5 copy.74
  7.0 7.7 %reshape.301 = f32[16,1,6912]{2,1,0:T(1,128)} reshape(f32[192,6,2,4,12]{4,3,2,1,0:T(4,128)} %bitcast.136) | data formatting | bytes 884736
  14.7 15.9 %all-to-all-start = ((f32[16,1,6912]{2,1,0:T(1,128)}), f32[16,1,6912]{2,1,0:T(1,128)S(1)}, u32[]{:S(2)}, u32[]{:S(2)}) async-start(f32[16,1,6912]{2,1,0:T(1,128)} %reshape.301), calls=%async_computation | async-start | bytes 884736 | tf_op jit(solution)/shard_map/all_to_all | solution.py:70
  30.6 0.1 convert_multiply_fusion.1
  30.7 0.1 convert_multiply_fusion.2
  30.8 0.1 fusion.13
  30.9 20.2 %all-to-all-done = f32[16,1,6912]{2,1,0:T(1,128)S(1)} async-done(((f32[16,1,6912]{2,1,0:T(1,128)}), f32[16,1,6912]{2,1,0:T(1,128)S(1)}, u32[]{:S(2)}, u32[]{:S(2)}) %all-to-all-start) | async-done | bytes 442400 | tf_op jit(solution)/shard_map/all_to_all | solution.py:70
  51.1 0.5 broadcast.423
  51.6 1.7 reduce.6
  53.3 7.8 %reshape.302 = f32[192,6,2,4,12]{4,3,2,1,0:T(4,128)} reshape(f32[16,6912]{1,0:T(8,128)S(1)} %reduce.6) | data formatting | bytes 884736
  61.0 7.2 %copy.163 = f32[4,6,12,2,16,12]{2,4,3,5,1,0:T(8,128)} copy(f32[4,6,12,2,16,12]{2,0,3,1,5,4:T(4,128)} %bitcast.137) | data formatting | bytes 884736 | tf_op jit(solution)/shard_map/all_to_all | solution.py:70
  68.3 4.3 %all_to_all.55 = f32[4,6,192,2,12]{2,3,4,1,0:T(2,128)S(1)} reshape(f32[4,6,16,12,2,12]{3,2,4,5,1,0:T(8,128)} %bitcast.138) | data formatting | bytes 884736 | tf_op jit(solution)/shard_map/all_to_all | solution.py:70
  72.6 1.5 convolution_bitcast_fusion.3
  74.1 4.8 %copy.79 = f32[4,6,12,2,192]{2,3,1,0,4:T(2,128)} copy(f32[4,6,12,2,192]{4,2,3,1,0:T(8,128)S(1)} %convolution_bitcast_fusion.3) | data formatting | bytes 884736 | tf_op jit(solution)/shard_map/bacrk,crsf->baksf/dot_general | solution.py:68
  78.9 8.6 %reshape.303 = f32[32,1,3456]{2,1,0:T(1,128)} reshape(f32[192,4,6,2,12]{4,3,2,1,0:T(2,128)} %bitcast.139) | data formatting | bytes 884736
  87.5 14.1 %all-to-all-start.1 = ((f32[32,1,3456]{2,1,0:T(1,128)}), f32[32,1,3456]{2,1,0:T(1,128)S(1)}, u32[]{:S(2)}, u32[]{:S(2)}) async-start(f32[32,1,3456]{2,1,0:T(1,128)} %reshape.303), calls=%async_computation.1 | async-start | bytes 884736 | tf_op jit(solution)/shard_map/all_to_all | solution.py:76
  101.6 0.1 broadcast_add_fusion
  101.7 0.1 fusion.36
  101.7 10.5 %all-to-all-done.1 = f32[32,1,3456]{2,1,0:T(1,128)S(1)} async-done(((f32[32,1,3456]{2,1,0:T(1,128)}), f32[32,1,3456]{2,1,0:T(1,128)S(1)}, u32[]{:S(2)}, u32[]{:S(2)}) %all-to-all-start.1) | async-done | bytes 442400 | tf_op jit(solution)/shard_map/all_to_all | solution.py:76
  112.2 1.7 reduce.7
  113.9 8.9 %reshape.304 = f32[192,4,6,2,12]{4,3,2,1,0:T(2,128)} reshape(f32[32,3456]{1,0:T(8,128)S(1)} %reduce.7) | data formatting | bytes 884736
  122.9 6.1 %copy.81 = f32[4,32,6,12,2,6]{3,4,5,2,1,0:T(2,128)} copy(f32[4,32,6,12,2,6]{3,4,2,0,5,1:T(2,128)} %bitcast.140) | data formatting | bytes 884736 | tf_op jit(solution)/shard_map/all_to_all | solution.py:76
  129.0 6.3 %copy.107 = f32[4,192,12,2,6,1]{1,4,3,5,2,0:T(8,128)S(1)} copy(f32[4,192,12,2,6,1]{2,3,4,1,0,5:T(2,128)} %bitcast.141) | data formatting | bytes 884736 | tf_op jit(solution)/shard_map/all_to_all | solution.py:76
  135.3 3.0 fusion.1
  138.3 3.0 convolution_bitcast_fusion
  141.3 3.7 %copy.85 = f32[4,12,6,2,192]{1,0,3,2,4:T(4,128)} copy(f32[4,12,6,2,192]{4,2,3,1,0:T(8,128)S(1)} %convolution_bitcast_fusion) | data formatting | bytes 884736 | tf_op jit(solution)/shard_map/bkftg,gtsa->bkfsa/dot_general | solution.py:81
  145.0 7.2 %reshape.305 = f32[32,1,3456]{2,1,0:T(1,128)S(1)} reshape(f32[192,6,2,4,12]{4,3,2,1,0:T(4,128)} %bitcast.142) | data formatting | bytes 884736
  152.2 14.1 %all_to_all.72 = f32[32,1,3456]{2,1,0:T(1,128)S(1)} all-to-all(f32[32,1,3456]{2,1,0:T(1,128)S(1)} %reshape.305), channel_id=1, replica_groups=mesh['slab'=32,'pencil'=16] {'slab'}, dimensions={0} | all-to-all | bytes 884736 | tf_op jit(solution)/shard_map/all_to_all | solution.py:82
  166.4 1.7 reduce.8
  168.1 7.8 %reshape.306 = f32[192,6,2,4,12]{4,3,2,1,0:T(4,128)} reshape(f32[32,3456]{1,0:T(8,128)S(1)} %reduce.8) | data formatting | bytes 884736
  175.8 4.8 %copy.86 = f32[4,12,6,2,192]{1,3,4,2,0:T(2,128)S(1)} copy(f32[4,12,6,2,192]{1,0,3,2,4:T(4,128)} %bitcast.143) | data formatting | bytes 884736 | tf_op jit(solution)/shard_map/all_to_all | solution.py:82
  180.6 3.7 %copy.87 = f32[4,12,32,6,2,6]{1,4,5,3,2,0:T(2,128)} copy(f32[4,12,32,6,2,6]{1,4,5,2,3,0:T(2,128)S(1)} %bitcast.144) | data formatting | bytes 884736 | tf_op jit(solution)/shard_map/all_to_all | solution.py:82
  184.3 6.3 %copy.113 = f32[4,12,192,2,6,1]{2,4,3,5,1,0:T(8,128)S(1)} copy(f32[4,12,192,2,6,1]{1,3,4,2,0,5:T(2,128)} %bitcast.145) | data formatting | bytes 884736 | tf_op jit(solution)/shard_map/all_to_all | solution.py:82
  190.6 3.0 convolution_bitcast_fusion.1
  193.6 0.0 copy-start.2
  193.6 3.7 %copy.90 = f32[4,12,6,2,192]{1,0,3,2,4:T(4,128)} copy(f32[4,12,6,2,192]{4,2,3,1,0:T(8,128)S(1)} %convolution_bitcast_fusion.1) | data formatting | bytes 884736 | tf_op jit(solution)/shard_map/bkfsa,fsrc->bkarc/dot_general | solution.py:83
  197.4 7.9 %reshape.307 = f32[16,1,6912]{2,1,0:T(1,128)} reshape(f32[192,6,2,4,12]{4,3,2,1,0:T(4,128)} %bitcast.146) | data formatting | bytes 884736
  205.3 5.6 %all-to-all-start.3 = ((f32[16,1,6912]{2,1,0:T(1,128)}), f32[16,1,6912]{2,1,0:T(1,128)S(1)}, u32[]{:S(2)}, u32[]{:S(2)}) async-start(f32[16,1,6912]{2,1,0:T(1,128)} %reshape.307), calls=%async_computation.3 | async-start | bytes 884736 | tf_op jit(solution)/shard_map/all_to_all | solution.py:84
  210.9 0.0 copy-done.2
  210.9 21.6 %all-to-all-done.3 = f32[16,1,6912]{2,1,0:T(1,128)S(1)} async-done(((f32[16,1,6912]{2,1,0:T(1,128)}), f32[16,1,6912]{2,1,0:T(1,128)S(1)}, u32[]{:S(2)}, u32[]{:S(2)}) %all-to-all-start.3) | async-done | bytes 442400 | tf_op jit(solution)/shard_map/all_to_all | solution.py:84
  232.5 1.7 reduce.9
  234.2 7.8 %reshape.308 = f32[192,6,2,4,12]{4,3,2,1,0:T(4,128)} reshape(f32[16,6912]{1,0:T(8,128)S(1)} %reduce.9) | data formatting | bytes 884736
  242.0 7.2 %copy.162 = f32[4,12,6,2,16,12]{1,4,3,5,2,0:T(8,128)} copy(f32[4,12,6,2,16,12]{1,0,3,2,5,4:T(4,128)} %bitcast.147) | data formatting | bytes 884736 | tf_op jit(solution)/shard_map/all_to_all | solution.py:84
  249.2 0.0 copy-start
  249.2 0.0 copy-start.1
  249.2 4.4 %all_to_all.67 = f32[4,192,6,2,12]{1,3,4,2,0:T(2,128)S(1)} reshape(f32[4,16,12,6,2,12]{2,1,4,5,3,0:T(8,128)} %bitcast.148) | data formatting | bytes 884736 | tf_op jit(solution)/shard_map/all_to_all | solution.py:84
  253.6 0.0 copy-done
  253.6 0.0 copy-done.1
  253.6 0.9 fusion.6
  254.6 1.4 fusion.7
  255.9 0.2 reshape.282
  256.1 105.4 %psum.7 = f32[4,4]{0,1:T(4,128)S(1)} all-reduce(f32[4,4]{0,1:T(4,128)S(1)} %fusion.7), channel_id=1, replica_groups=mesh['slab'=32,'pencil'=16] {'slab','pencil'}, use_global_device_ids=true, to_apply=%region_0.1 | all-reduce | flops 16 | bytes 128 | tf_op jit(solution)/shard_map/psum | solution.py:96
  361.5 0.1 copy.100
  361.6 0.4 cholesky.16
  362.0 0.6 compare_reduce_fusion
  362.7 0.6 fusion.39
  363.3 0.3 custom-call.7
  363.7 0.2 triangular_solve.39
  363.9 1.6 fusion.19
  (5 shorter events, 0.0 us)
Async XLA Ops:
  14.7 36.4 %all-to-all-start = ((f32[16,1,6912]{2,1,0:T(1,128)}), f32[16,1,6912]{2,1,0:T(1,128)S(1)}, u32[]{:S(2)}, u32[]{:S(2)}) async-start(f32[16,1,6912]{2,1,0:T(1,128)} %reshape.301), calls=%async_computation | async-start | bytes 884736 | tf_op jit(solution)/shard_map/all_to_all | solution.py:70
  87.5 24.7 %all-to-all-start.1 = ((f32[32,1,3456]{2,1,0:T(1,128)}), f32[32,1,3456]{2,1,0:T(1,128)S(1)}, u32[]{:S(2)}, u32[]{:S(2)}) async-start(f32[32,1,3456]{2,1,0:T(1,128)} %reshape.303), calls=%async_computation.1 | async-start | bytes 884736 | tf_op jit(solution)/shard_map/all_to_all | solution.py:76
  193.6 17.3 %copy-start.2 = (s32[4]{0:T(128)S(1)}, s32[4]{0:T(128)}, u32[]{:S(2)}) copy-start(s32[4]{0:T(128)} %param.5) | copy-start | bytes 52
  205.3 27.3 %all-to-all-start.3 = ((f32[16,1,6912]{2,1,0:T(1,128)}), f32[16,1,6912]{2,1,0:T(1,128)S(1)}, u32[]{:S(2)}, u32[]{:S(2)}) async-start(f32[16,1,6912]{2,1,0:T(1,128)} %reshape.307), calls=%async_computation.3 | async-start | bytes 884736 | tf_op jit(solution)/shard_map/all_to_all | solution.py:84
  249.2 4.4 %copy-start = (f32[4,6,12,192]{3,0,2,1:T(4,128)S(1)}, f32[4,6,12,192]{3,0,2,1:T(4,128)}, u32[]{:S(2)}) copy-start(f32[4,6,12,192]{3,0,2,1:T(4,128)} %param.3) | copy-start | bytes 663556
  249.2 4.4 %copy-start.1 = (f32[6,12,192]{2,1,0:T(8,128)S(1)}, f32[6,12,192]{2,1,0:T(8,128)}, u32[]{:S(2)}) copy-start(f32[6,12,192]{2,1,0:T(8,128)} %param.4) | copy-start | bytes 165892
where the time goes:
time: 371 us; the launch traced here: 366 us
  local copies, waits for them, and re-layouts  131 us (35%)
  blocking collectives  120 us (32%)
  waiting for transfers between devices  52.3 us (14%)
  starting transfers between devices  35.6 us (10%)
  matrix products  16.2 us (4%)
  other arithmetic  10.9 us (3%)
    psum x1, blocking collectives, local(): intersection = lax.psum(partial_intersection, ('slab', 'pencil'))  105 us
    unnamed x14, local copies, waits for them, and re-layouts  63.6 us
    all_to_all x1, waiting for transfers between devices, local(): lax.all_to_all(rows_c, 'pencil', split_axis=4, concat_axis=1, tiled=True)  21.6 us
    all_to_all x1, waiting for transfers between devices, local(): lax.all_to_all(lines_k, 'pencil', split_axis=4, concat_axis=2, tiled=True)  20.2 us
    all_to_all x1, starting transfers between devices, local(): lax.all_to_all(lines_k, 'pencil', split_axis=4, concat_axis=2, tiled=True)  15.9 us
    all_to_all x3, local copies, waits for them, and re-layouts, local(): lax.all_to_all(along_a, 'slab', split_axis=4, concat_axis=2, tiled=True)  14.8 us
    all_to_all x1, blocking collectives, local(): lax.all_to_all(along_a, 'slab', split_axis=4, concat_axis=2, tiled=True)  14.1 us
    all_to_all x1, starting transfers between devices, local(): lax.all_to_all(along_f, 'slab', split_axis=4, concat_axis=1, tiled=True)  14.1 us
  transfers between devices with their start and end apart: 3, of which 3 were waited for; matrix products, arithmetic and copies ran while one was open for 0% of the time, Pallas kernels for 0%

commit v1 on v0

v1 whole, which is shorter than its diff:
```python
import functools

import jax
import jax.numpy as jnp
import numpy as np
from jax import lax
from jax.experimental import pallas as pl
from jax.experimental.pallas import tpu as pltpu
from jax.sharding import PartitionSpec as P

NG = 192
NB = 4
CUT = NG // 4
MODES = 2 * CUT
SLAB = 32
PENCIL = 16
ROWS = NG // SLAB
COLS = NG // PENCIL
CELLS = float(NG**3)
THIRDS = MODES // SLAB
FIRSTS = MODES // PENCIL
PAIRS = [(a, b) for a in range(NB) for b in range(a + 1)]
highest = lax.Precision.HIGHEST


def basis():
    place = np.arange(NG)
    mode = np.arange(MODES)
    angle = 2.0 * np.pi / NG * ((mode[:, None] % CUT) * place[None, :] % NG)
    return np.where(mode[:, None] < CUT, np.cos(angle), np.sin(angle))


def tables():
    real = basis()
    third = real
    first = np.zeros((PENCIL, 8, SLAB, 8))
    first[:, :FIRSTS, :, :ROWS] = real.reshape(PENCIL, FIRSTS, SLAB, ROWS)
    first = first.reshape(PENCIL * 8, SLAB * 8)
    second = np.zeros((128, PENCIL, 16))
    second[:MODES, :, :COLS] = real.reshape(MODES, PENCIL, COLS)
    second = second.reshape(128, PENCIL * 16)
    third_back = real.reshape(SLAB, THIRDS, NG).transpose(1, 0, 2).reshape(MODES, NG)
    made = (third, first, first.T, second.T, second, third_back)
    return [np.ascontiguousarray(t, dtype=np.float32) for t in made]


def dot(a, b, dims=((1,), (0,))):
    return lax.dot_general(a, b, (dims, ((), ())), precision=highest, preferred_element_type=jnp.float32)


def local_part(flag, orbital, shifted):
    return jnp.where(flag == 1, orbital * shifted * (1.0 / 1.5), orbital)


def forward_third(flags, orbitals, potential, table, out, sums, lines):
    empty = jnp.zeros((16 - COLS, NG), jnp.float32)
    totals = [None] * len(PAIRS)
    for i in range(ROWS):
        shifted = potential[i] - 1.0
        for b in range(NB):
            base = i * 128 + b * 16
            value = orbitals[b, i]
            lines[base : base + COLS, :] = value
            lines[base + COLS : base + 16, :] = empty
            lines[base + 64 : base + 64 + COLS, :] = local_part(flags[b], value, shifted)
            lines[base + 64 + COLS : base + 80, :] = empty
        own = [lines[i * 128 + 64 + b * 16 : i * 128 + 80 + b * 16, :] for b in range(NB)]
        for q, (a, b) in enumerate(PAIRS):
            term = own[a] * own[b]
            totals[q] = term if totals[q] is None else totals[q] + term
    for q in range(len(PAIRS)):
        sums[q * 8 : q * 8 + 8, :] = totals[q][:8] + totals[q][8:]
    spectrum = dot(table[...], lines[...], ((1,), (1,)))
    for i in range(ROWS):
        out[pl.ds(i, MODES, stride=8), :] = spectrum[:, i * 128 : i * 128 + 128]
    for i in range(ROWS, 8):
        out[pl.ds(i, MODES, stride=8), :] = jnp.zeros((MODES, 128), jnp.float32)


def forward_first(given, table, out):
    for t in range(THIRDS):
        block = given[:, t * 8 : t * 8 + 8, :].reshape(SLAB * 8, 128)
        out[:, t * 8 : t * 8 + 8, :] = dot(table[...], block).reshape(PENCIL, 8, 128)


def middle(flags, places, given, sums, forward, back, out, lines):
    for p in range(PENCIL):
        for u in range(2 * NB):
            lines[u * 24 : u * 24 + 24, p * 16 : p * 16 + 16] = given[p, :, u * 16 : u * 16 + 16]
    spectrum = dot(lines[...], forward[...])
    row = lax.broadcasted_iota(jnp.int32, (24, 128), 0)
    lane = lax.broadcasted_iota(jnp.int32, (24, 128), 1)
    third = THIRDS * places[0] + row // 8
    first = FIRSTS * places[1] + row % 8
    known = (row % 8 < FIRSTS) & (lane < MODES)
    squared = jnp.zeros((24, 128), jnp.int32)
    weight = jnp.full((24, 128), 1.0 / CELLS, jnp.float32)
    for mode in (third, first, lane):
        size = jnp.where(mode < CUT, mode, mode - CUT)
        squared = squared + size * size
        weight = weight * jnp.where(mode == 0, 1.0, jnp.where(mode == CUT, 0.0, 2.0))
    kinetic = squared.astype(jnp.float32) * (4.0 / CUT**2)
    kinetic = jnp.where(known & (squared < CUT * CUT), kinetic, 0.0)
    weight = weight * kinetic
    scaled, other = [], []
    for b in range(NB):
        alpha = jnp.where(flags[b] == 1, 1.0 / 1.5, 0.0)
        value = spectrum[b * 24 : b * 24 + 24] * alpha
        scaled.append(value * weight)
        other.append(0.5 * kinetic * value + spectrum[(NB + b) * 24 : (NB + b) * 24 + 24])
    returned = dot(jnp.concatenate(scaled, axis=0), back[...])
    for p in range(PENCIL):
        for b in range(NB):
            for t in range(THIRDS):
                at = (t % 2) * 64 + b * 16
                out[p, (t // 2) * 8 : (t // 2) * 8 + 8, at : at + 16] = returned[
                    b * 24 + t * 8 : b * 24 + t * 8 + 8, p * 16 : p * 16 + 16
                ]
    values = []
    for q, (a, b) in enumerate(PAIRS):
        term = scaled[a] * other[b] + scaled[b] * other[a]
        term = term[:8] + term[8:16] + term[16:]
        mine = sums[q * 8 : q * 8 + 8, :]
        total = jnp.sum(term, axis=1, keepdims=True) + jnp.sum(mine, axis=1, keepdims=True)
        values.append(jnp.sum(total, axis=0, keepdims=True))
    row = lax.broadcasted_iota(jnp.int32, (8, 64), 0)
    lane = lax.broadcasted_iota(jnp.int32, (8, 64), 1)
    note = jnp.zeros((8, 64), jnp.float32)
    for q, value in enumerate(values):
        note = jnp.where((row == q % 8) & (lane == q // 8), value, note)
    for p in range(PENCIL):
        out[p, 8:16, 64:128] = note


def back_first(given, table, out):
    low = given[:, 0:8, :].reshape(PENCIL * 8, 128)
    high = given[:, 8:16, :].reshape(PENCIL * 8, 128)
    note = given[0, 8:16, :]
    for p in range(1, PENCIL):
        note = note + given[p, 8:16, :]
    out[:, 0:8, :] = dot(table[...], low).reshape(SLAB, 8, 128)
    lane = lax.broadcasted_iota(jnp.int32, (SLAB, 8, 128), 2)
    out[:, 8:16, :] = jnp.where(lane >= 64, note[None], dot(table[...], high).reshape(SLAB, 8, 128))


def back_third(flags, orbitals, potential, given, table, out, lines):
    for i in range(ROWS):
        low = given[pl.ds(i, SLAB, stride=16), :]
        high = given[pl.ds(8 + i, SLAB, stride=16), :]
        lines[0:32, i * 64 : i * 64 + 64] = low[:, :64]
        lines[32:64, i * 64 : i * 64 + 64] = low[:, 64:]
        lines[64:96, i * 64 : i * 64 + 64] = high[:, :64]
    kinetic_part = dot(lines[...], table[...], ((0,), (0,)))
    note = given[8:16, :]
    for s in range(1, SLAB):
        note = note + given[s * 16 + 8 : s * 16 + 16, :]
    note = note * (1.0 / CELLS)
    entry = {}
    for q, pair in enumerate(PAIRS):
        at = 64 + q // 8
        entry[pair] = note[q % 8 : q % 8 + 1, at : at + 1]
    factor, inverse = {}, {}
    for a in range(NB):
        for b in range(a + 1):
            value = entry[a, b]
            for c in range(b):
                value = value - factor[a, c] * factor[b, c]
            if a == b:
                factor[a, a] = jnp.sqrt(value)
                inverse[a] = 1.0 / factor[a, a]
            else:
                factor[a, b] = value * inverse[b]
    for i in range(ROWS):
        shifted = potential[i] - 1.0
        done = []
        for a in range(NB):
            value = local_part(flags[a], orbitals[a, i], shifted)
            value = value + kinetic_part[i * 64 + a * 16 : i * 64 + a * 16 + COLS]
            for b in range(a):
                value = value - factor[a, b] * done[b]
            value = value * inverse[a]
            done.append(value)
            out[a, i] = value


def smem():
    return pl.BlockSpec(memory_space=pltpu.SMEM)


def vmem():
    return pl.BlockSpec(memory_space=pltpu.VMEM)


def f32(*shape):
    return jax.ShapeDtypeStruct(shape, jnp.float32)


def call(body, kinds, outs, scratch=()):
    return pl.pallas_call(
        body,
        out_shape=outs,
        in_specs=[smem() if kind == "s" else vmem() for kind in kinds],
        out_specs=jax.tree.map(lambda _: vmem(), outs),
        scratch_shapes=[pltpu.VMEM(shape, jnp.float32) for shape in scratch],
        name=body.__name__,
    )


def steps():
    third, first, first_back, second, second_back, third_back = tables()

    def one(flags, orbitals, potential):
        made = call(forward_third, "svvv", (f32(MODES * 8, 128), f32(8 * len(PAIRS), NG)), [(ROWS * 128, NG)])
        spectrum, sums = made(flags, orbitals, potential, third)
        return spectrum.reshape(SLAB, 24, 128), sums

    def two(given):
        return call(forward_first, "vv", f32(PENCIL, 24, 128))(given, first)

    def three(flags, places, given, sums):
        made = call(middle, "ssvvvv", f32(PENCIL, 16, 128), [(8 * 24, PENCIL * 16)])
        return made(flags, places, given, sums, second, second_back)

    def four(given):
        return call(back_first, "vv", f32(SLAB, 16, 128))(given, first_back)

    def five(flags, orbitals, potential, given):
        made = call(back_third, "svvvv", f32(NB, ROWS, COLS, NG), [(MODES, ROWS * 64)])
        return made(flags, orbitals, potential, given.reshape(SLAB * 16, 128), third_back)

    return one, two, three, four, five


def local(orbitals, potential, unlocked):
    one, two, three, four, five = steps()
    trade = functools.partial(lax.all_to_all, split_axis=0, concat_axis=0, tiled=True)
    places = jnp.stack([lax.axis_index("slab"), lax.axis_index("pencil")]).astype(jnp.int32)
    spectrum, sums = one(unlocked, orbitals, potential)
    spectrum = two(trade(spectrum, "slab"))
    spectrum = three(unlocked, places, trade(spectrum, "pencil"), sums)
    spectrum = four(trade(spectrum, "pencil"))
    return five(unlocked, orbitals, potential, trade(spectrum, "slab"))


def solution(mesh):
    in_specs = (P(None, "slab", "pencil", None), P("slab", "pencil", None), P())
    out_specs = P(None, "slab", "pencil", None)
    return jax.shard_map(local, mesh=mesh, in_specs=in_specs, out_specs=out_specs, check_vma=False)
```

time: 371 us -> 102 us (0.27); the launches traced: 366 us -> 101 us
  local copies, waits for them, and re-layouts: 131 us -> 4.35 us
  blocking collectives: 120 us -> 58.5 us
  waiting for transfers between devices: 52.3 us -> 12.7 us
  starting transfers between devices: 35.6 us -> 12.4 us
  matrix products: 16.2 us -> 0 us
  Pallas kernels: 0 us -> 12.5 us
  other arithmetic: 10.9 us -> 0.58 us
    psum x1 -> x0, blocking collectives: 105 us -> none  [local(): intersection = lax.psum(partial_intersection, ('slab', 'pencil'))]
    unnamed x14 -> x3, local copies, waits for them, and re-layouts: 63.6 us -> 2.45 us
    all_to_all x10 -> x0, local copies, waits for them, and re-layouts: 50.9 us -> none  [the longest x3 14.8 us: local(): lax.all_to_all(along_a, 'slab', split_axis=4, concat_axis=2, tiled=True)]
    all_to_all x1 -> x3, blocking collectives: 14.1 us -> 58.5 us  [the longest x1 21.4 us: local(): spectrum = two(trade(spectrum, 'slab'))]
    all_to_all x3 -> x1, waiting for transfers between devices: 52.3 us -> 12.7 us  [local(): spectrum = three(unlocked, places, trade(spectrum, 'pencil'), sums)]
    all_to_all x3 -> x1, starting transfers between devices: 35.6 us -> 12.4 us  [local(): spectrum = three(unlocked, places, trade(spectrum, 'pencil'), sums)]
    dot_general x4 -> x0, local copies, waits for them, and re-layouts: 15.9 us -> none  [the longest x1 4.85 us: local(): jnp.einsum('bacrk,crsf->baksf', lax.all_to_all(lines_k, 'pencil', split_a...]
    dot_general x7 -> x0, matrix products: 14.6 us -> none  [the longest x1 3.01 us: local(): jnp.einsum('baksf,astg->bkftg', lax.all_to_all(along_f, 'slab', split_axi...]
  transfers between devices with their start and end apart: 3 -> 1, of which waited for: 3 -> 1; matrix products, arithmetic and copies ran while one was open for 0% -> 1% of each run, Pallas kernels for 0% -> 0%
where the time goes in v1:
time: 102 us; the launch traced here: 101 us
  blocking collectives  58.5 us (57%)
  waiting for transfers between devices  12.7 us (12%)
  Pallas kernels  12.5 us (12%)
  starting transfers between devices  12.4 us (12%)
  local copies, waits for them, and re-layouts  4.35 us (4%)
    all_to_all x1, blocking collectives, local(): spectrum = two(trade(spectrum, 'slab'))  21.4 us
    all_to_all x1, blocking collectives, local(): spectrum = four(trade(spectrum, 'pencil'))  20.4 us
    all_to_all x1, blocking collectives, local(): return five(unlocked, orbitals, potential, trade(spectrum, 'slab'))  16.6 us
    all_to_all x1, waiting for transfers between devices, local(): spectrum = three(unlocked, places, trade(spectrum, 'pencil'), sums)  12.7 us
    all_to_all x1, starting transfers between devices, local(): spectrum = three(unlocked, places, trade(spectrum, 'pencil'), sums)  12.4 us
    pallas_call x1, Pallas kernels, three(): return made(flags, places, given, sums, second, second_back)  3 us
    pallas_call x1, Pallas kernels, one(): spectrum, sums = made(flags, orbitals, potential, third)  2.8 us
    pallas_call x1, Pallas kernels, five(): made(flags, orbitals, potential, given.reshape(SLAB * 16, 128), third_back)  2.54 us
  transfers between devices with their start and end apart: 1, of which 1 were waited for; matrix products, arithmetic and copies ran while one was open for 1% of the time, Pallas kernels for 0%

profile of v1, /device:TPU:1, one launch (start us, length us, event | category | flops | bytes accessed | tf_op | source)
XLA Modules:
  0.0 101.0 jit_solution(6212261323045388377)
XLA Ops:
  0.0 1.8 %copy.11.orbitals = f32[4,6,12,192]{3,2,1,0:T(8,128)} copy(f32[4,6,12,192]{3,0,2,1:T(4,128)} %param.9) | data formatting | bytes 442368 | tf_op args[0]
  1.8 2.8 %forward_third.1 = (f32[768,128]{1,0:T(8,128)}, f32[80,192]{1,0:T(8,128)}) custom-call(s32[4]{0:T(128)} %flags.5, f32[4,6,12,192]{3,2,1,0:T(8,128)} %copy.11.orbitals, f32[6,12,192]{2,1,0:T(8,128)} %potential.3, f32[96,192]{1,0:T(8,128)} %constant.21.clone.table), custom_call_target="tpu_custom_call" | custom-call | tf_op jit(solution)/shard_map/forward_third/pallas_call | solution.py:214
  4.6 21.4 %all_to_all.20.given = f32[32,24,128]{2,1,0:T(8,128)} all-to-all(f32[32,24,128]{2,1,0:T(8,128)} %bitcast.5), channel_id=1, replica_groups=mesh['slab'=32,'pencil'=16] {'slab'}, dimensions={0} | all-to-all | bytes 786432 | tf_op jit(solution)/shard_map/all_to_all | solution.py:239
  26.0 2.2 %forward_first.1 = f32[16,24,128]{2,1,0:T(8,128)} custom-call(f32[32,24,128]{2,1,0:T(8,128)} %all_to_all.20.given, f32[128,256]{1,0:T(8,128)} %constant.22.clone.table), custom_call_target="tpu_custom_call" | custom-call | tf_op jit(solution)/shard_map/forward_first/pallas_call | solution.py:218
  28.2 12.4 %all-to-all-start.1 = ((f32[16,24,128]{2,1,0:T(8,128)}), f32[16,24,128]{2,1,0:T(8,128)S(1)}, u32[]{:S(2)}, u32[]{:S(2)}) async-start(f32[16,24,128]{2,1,0:T(8,128)} %forward_first.1), calls=%async_computation.1 | async-start | bytes 393216 | tf_op jit(solution)/shard_map/all_to_all | solution.py:240
  40.6 0.6 pad_add_fusion.places
  41.2 12.7 %all-to-all-done.1.given = f32[16,24,128]{2,1,0:T(8,128)S(1)} async-done(((f32[16,24,128]{2,1,0:T(8,128)}), f32[16,24,128]{2,1,0:T(8,128)S(1)}, u32[]{:S(2)}, u32[]{:S(2)}) %all-to-all-start.1) | async-done | bytes 196640 | tf_op jit(solution)/shard_map/all_to_all | solution.py:240
  53.9 0.0 copy-start
  53.9 0.7 copy-done
  54.6 3.0 %middle.1 = f32[16,16,128]{2,1,0:T(8,128)} custom-call(s32[4]{0:T(128)} %flags.5, s32[2]{0:T(128)} %pad_add_fusion.places, f32[16,24,128]{2,1,0:T(8,128)} %copy-done, f32[80,192]{1,0:T(8,128)} %get-tuple-element.8.sums, f32[256,128]{1,0:T(8,128)} %constant.23.clone.forward, f32[128,256]{1,0:T(8,128)} %constant.24.clone.back), custom_call_target="tpu_custom_call" | custom-call | tf_op jit(solution)/shard_map/middle/pallas_call | solution.py:222
  57.6 20.4 %all_to_all.21.given = f32[16,16,128]{2,1,0:T(8,128)} all-to-all(f32[16,16,128]{2,1,0:T(8,128)} %middle.1), channel_id=1, replica_groups=mesh['slab'=32,'pencil'=16] {'pencil'}, dimensions={0} | all-to-all | bytes 262144 | tf_op jit(solution)/shard_map/all_to_all | solution.py:241
  77.9 2.0 %back_first.1 = f32[32,16,128]{2,1,0:T(8,128)} custom-call(f32[16,16,128]{2,1,0:T(8,128)} %all_to_all.21.given, f32[256,128]{1,0:T(8,128)} %constant.25.clone.table), custom_call_target="tpu_custom_call" | custom-call | tf_op jit(solution)/shard_map/back_first/pallas_call | solution.py:225
  80.0 16.6 %all_to_all.22 = f32[32,16,128]{2,1,0:T(8,128)} all-to-all(f32[32,16,128]{2,1,0:T(8,128)} %back_first.1), channel_id=1, replica_groups=mesh['slab'=32,'pencil'=16] {'slab'}, dimensions={0} | all-to-all | bytes 524288 | tf_op jit(solution)/shard_map/all_to_all | solution.py:242
  96.6 2.5 %back_third.1 = f32[4,6,12,192]{3,2,1,0:T(8,128)} custom-call(s32[4]{0:T(128)} %flags.5, f32[4,6,12,192]{3,2,1,0:T(8,128)} %copy.11.orbitals, f32[6,12,192]{2,1,0:T(8,128)} %potential.3, f32[512,128]{1,0:T(8,128)} %bitcast.4, f32[96,192]{1,0:T(8,128)} %constant.26.clone.table), custom_call_target="tpu_custom_call" | custom-call | tf_op jit(solution)/shard_map/back_third/pallas_call | solution.py:229
  99.1 1.9 %copy.12 = f32[4,6,12,192]{3,0,2,1:T(4,128)} copy(f32[4,6,12,192]{3,2,1,0:T(8,128)} %back_third.1) | data formatting | bytes 442368 | tf_op jit(solution)/shard_map/back_third/pallas_call | solution.py:229
Async XLA Ops:
  28.2 25.7 %all-to-all-start.1 = ((f32[16,24,128]{2,1,0:T(8,128)}), f32[16,24,128]{2,1,0:T(8,128)S(1)}, u32[]{:S(2)}, u32[]{:S(2)}) async-start(f32[16,24,128]{2,1,0:T(8,128)} %forward_first.1), calls=%async_computation.1 | async-start | bytes 393216 | tf_op jit(solution)/shard_map/all_to_all | solution.py:240
  53.9 0.7 copy-start

commit v2 on v1

v2 whole, which is shorter than its diff:
```python
import functools

import jax
import jax.numpy as jnp
import numpy as np
from jax import lax
from jax.experimental import pallas as pl
from jax.experimental.pallas import tpu as pltpu
from jax.sharding import PartitionSpec as P

NG = 192
NB = 4
CUT = NG // 4
MODES = 2 * CUT
SLAB = 32
PENCIL = 16
ROWS = NG // SLAB
COLS = NG // PENCIL
CELLS = float(NG**3)
THIRDS = MODES // SLAB
FIRSTS = MODES // PENCIL
WIDE = 2 * NB * COLS
HALF = NB * COLS
PAIRS = [(a, b) for a in range(NB) for b in range(a + 1)]
highest = lax.Precision.HIGHEST


def basis():
    place = np.arange(NG)
    mode = np.arange(MODES)
    angle = 2.0 * np.pi / NG * ((mode[:, None] % CUT) * place[None, :] % NG)
    return np.where(mode[:, None] < CUT, np.cos(angle), np.sin(angle))


def tables():
    real = basis()
    third = real.reshape(SLAB, THIRDS, NG).transpose(1, 0, 2).reshape(MODES, NG)
    first = np.zeros((PENCIL, 8, SLAB, 8))
    first[:, :FIRSTS, :, :ROWS] = real.reshape(PENCIL, FIRSTS, SLAB, ROWS)
    first = first.reshape(PENCIL * 8, SLAB * 8)
    second = np.zeros((128, NG))
    second[:MODES] = real
    made = (third, first, first.T, second.T, second)
    return [np.ascontiguousarray(t, dtype=np.float32) for t in made]


def dot(a, b, dims=((1,), (0,))):
    return lax.dot_general(a, b, (dims, ((), ())), precision=highest, preferred_element_type=jnp.float32)


def lanes(*shape):
    return lax.broadcasted_iota(jnp.int32, shape, len(shape) - 1)


def turn(value, by):
    by = by % 128
    return pltpu.roll(value, by, 1) if by else value


def gathered(pieces, width, start):
    lane = lanes(*pieces[0].shape)
    result = jnp.zeros(pieces[0].shape, jnp.float32)
    for k, piece in enumerate(pieces):
        here = (lane >= k * width) & (lane < k * width + width)
        result = jnp.where(here, turn(piece, k * width - start), result)
    return result


def forward_third(flags, orbitals, potential, table, out, local, sums, lines):
    totals = [None] * len(PAIRS)
    for i in range(ROWS):
        shifted = (potential[i] - 1.0) * (1.0 / 1.5)
        own = []
        for b in range(NB):
            base = i * 128 + b * COLS
            value = orbitals[i, :, b, :]
            kept = jnp.where(flags[b] == 1, value * shifted, value)
            lines[base : base + COLS, :] = value
            lines[base + HALF : base + HALF + COLS, :] = kept
            local[b, i] = kept
            own.append(kept)
        for q, (a, b) in enumerate(PAIRS):
            term = own[a] * own[b]
            totals[q] = term if totals[q] is None else totals[q] + term
    sums[...] = jnp.zeros_like(sums)
    for q in range(len(PAIRS)):
        sums[q : q + 1, :] = jnp.sum(totals[q], axis=0, keepdims=True)
    spectrum = dot(table[...], lines[...], ((1,), (1,)))
    whole = lanes(SLAB, 128)
    last = []
    for i in range(ROWS):
        parts = [spectrum[t * 32 : t * 32 + 32, i * 128 : i * 128 + 128] for t in range(THIRDS)]
        for t in range(2):
            extra = turn(parts[2], WIDE - 32 * t)
            out[pl.ds(t * 8 + i, SLAB, stride=16), :] = jnp.where(whole < WIDE, parts[t], extra)
        last.append(parts[2])
    for t in range(2):
        out[pl.ds(t * 8 + 6, SLAB, stride=16), :] = gathered(last[t * 4 : t * 4 + 4], 32, 64)
        out[pl.ds(t * 8 + 7, SLAB, stride=16), :] = jnp.zeros((SLAB, 128), jnp.float32)


def forward_first(given, table, out, taken, made):
    rest = [given[pl.ds(t * 8 + 6, SLAB, stride=16), :] for t in range(2)]
    for i in range(8):
        value = turn(rest[i // 4], -32 * (i % 4)) if i < ROWS else jnp.zeros((SLAB, 128), jnp.float32)
        taken[pl.ds(i, SLAB, stride=8), :] = value
    tiles = given[...].reshape(SLAB, 16, 128)
    for t in range(2):
        block = tiles[:, t * 8 : t * 8 + 8].reshape(SLAB * 8, 128)
        result = dot(table[...], block)
        for p in range(PENCIL):
            out[p * 16 + t * 8 : p * 16 + t * 8 + 8, :] = result[p * 8 : p * 8 + 8]
    made[...] = dot(table[...], taken[...])
    pieces = [made[pl.ds(i, PENCIL, stride=8), :] for i in range(FIRSTS)]
    for t in range(2):
        out[pl.ds(t * 8 + 6, PENCIL, stride=16), :] = gathered(pieces[t * 4 : t * 4 + 4], 32, 0)


def middle(flags, given, sums, forward, back, out, third, lines, wide, more, rows):
    rest = [given[pl.ds(t * 8 + 6, PENCIL, stride=16), :] for t in range(2)]
    for i in range(8):
        value = turn(rest[i // 4], 64 - 32 * (i % 4)) if i < FIRSTS else jnp.zeros((PENCIL, 128), jnp.float32)
        third[pl.ds(i, PENCIL, stride=8), :] = value
    lane = lanes(8, 128)
    for p in range(PENCIL):
        parts = [given[p * 16 : p * 16 + 8, :], given[p * 16 + 8 : p * 16 + 16, :]]
        last = jnp.where(lane < 64, turn(parts[1], 64), third[p * 8 : p * 8 + 8, :])
        parts.append(jnp.where(lane < 32, turn(parts[0], 32), last))
        for u in range(2 * NB):
            for t in range(THIRDS):
                at = u * 24 + t * 8
                lines[at : at + 8, p * COLS : p * COLS + COLS] = parts[t][:, u * COLS : u * COLS + COLS]
    spectrum = dot(lines[...], forward[...])
    row = lax.broadcasted_iota(jnp.int32, (24, 128), 0)
    lane = lanes(24, 128)
    third_mode = THIRDS * lax.axis_index("slab") + row // 8
    first_mode = FIRSTS * lax.axis_index("pencil") + row % 8
    known = (row % 8 < FIRSTS) & (lane < MODES)
    squared = jnp.zeros((24, 128), jnp.int32)
    weight = jnp.full((24, 128), 1.0 / CELLS, jnp.float32)
    for mode in (third_mode, first_mode, lane):
        size = jnp.where(mode < CUT, mode, mode - CUT)
        squared = squared + size * size
        weight = weight * jnp.where(mode == 0, 1.0, jnp.where(mode == CUT, 0.0, 2.0))
    kinetic = squared.astype(jnp.float32) * (4.0 / CUT**2)
    kinetic = jnp.where(known & (squared < CUT * CUT), kinetic, 0.0)
    weight = weight * kinetic
    scaled, other = [], []
    for b in range(NB):
        alpha = jnp.where(flags[b] == 1, 1.0 / 1.5, 0.0)
        value = spectrum[b * 24 : b * 24 + 24] * alpha
        scaled.append(value * weight)
        other.append(0.5 * kinetic * value + spectrum[(NB + b) * 24 : (NB + b) * 24 + 24])
    returned = dot(jnp.concatenate(scaled, axis=0), back[...])
    rows[...] = jnp.zeros_like(rows)
    for q, (a, b) in enumerate(PAIRS):
        term = scaled[a] * other[b] + scaled[b] * other[a]
        rows[q : q + 1, :] = jnp.sum(term[:8] + term[8:16] + term[16:], axis=0, keepdims=True)
    total = jnp.sum(rows[...], axis=1, keepdims=True) + jnp.sum(sums[...], axis=1, keepdims=True)
    picked = lax.broadcasted_iota(jnp.int32, (16, 128), 0) == lanes(16, 128)
    note = jnp.sum(jnp.where(picked, total, 0.0), axis=0, keepdims=True)
    for p in range(PENCIL):
        for b in range(NB):
            for t in range(THIRDS):
                at = t * HALF + b * COLS
                wide[p * 8 : p * 8 + 8, at : at + COLS] = returned[b * 24 + t * 8 : b * 24 + t * 8 + 8, p * COLS : p * COLS + COLS]
    more[...] = wide[:, 128:256]
    out[...] = wide[:, 0:128]
    pieces = [more[pl.ds(i, PENCIL, stride=8), :] for i in range(FIRSTS)]
    out[pl.ds(6, PENCIL, stride=8), :] = gathered(pieces, 16, 0)
    out[pl.ds(7, PENCIL, stride=8), :] = jnp.broadcast_to(note, (PENCIL, 128))


def back_first(given, table, out, taken, made):
    rest = given[pl.ds(6, PENCIL, stride=8), :]
    for i in range(8):
        value = turn(rest, -16 * i) if i < FIRSTS else jnp.zeros((PENCIL, 128), jnp.float32)
        taken[pl.ds(i, PENCIL, stride=8), :] = value
    out[...] = dot(table[...], given[...])
    made[...] = dot(table[...], taken[...])
    pieces = [made[pl.ds(i, SLAB, stride=8), :] for i in range(ROWS)]
    out[pl.ds(6, SLAB, stride=8), :] = gathered(pieces, 16, 0)
    note = jnp.sum(given[pl.ds(7, PENCIL, stride=8), :], axis=0, keepdims=True)
    out[pl.ds(7, SLAB, stride=8), :] = jnp.broadcast_to(note, (SLAB, 128))


def back_third(given, local, table, out, lines):
    rest = given[pl.ds(6, SLAB, stride=8), :]
    for i in range(ROWS):
        value = given[pl.ds(i, SLAB, stride=8), :]
        at = i * HALF
        lines[0:32, at : at + HALF] = value[:, :HALF]
        lines[32:64, at : at + HALF] = value[:, HALF:WIDE]
        lines[64:96, at : at + 32] = value[:, WIDE:128]
        lines[64:96, at + 32 : at + HALF] = rest[:, 16 * i : 16 * i + 16]
    kinetic_part = dot(lines[...], table[...], ((0,), (0,)))
    note = jnp.sum(given[pl.ds(7, SLAB, stride=8), :], axis=0, keepdims=True) * (1.0 / CELLS)
    factor, inverse = {}, {}
    for q, (a, b) in enumerate(PAIRS):
        value = note[:, q : q + 1]
        for c in range(b):
            value = value - factor[a, c] * factor[b, c]
        if a == b:
            factor[a, a] = jnp.sqrt(value)
            inverse[a] = 1.0 / factor[a, a]
        else:
            factor[a, b] = value * inverse[b]
    for i in range(ROWS):
        done = []
        for a in range(NB):
            value = local[a, i] + kinetic_part[i * HALF + a * COLS : i * HALF + a * COLS + COLS]
            for b in range(a):
                value = value - factor[a, b] * done[b]
            value = value * inverse[a]
            done.append(value)
            out[i, :, a, :] = value


def smem():
    return pl.BlockSpec(memory_space=pltpu.SMEM)


def vmem():
    return pl.BlockSpec(memory_space=pltpu.VMEM)


def f32(*shape):
    return jax.ShapeDtypeStruct(shape, jnp.float32)


def call(body, kinds, outs, scratch=()):
    return pl.pallas_call(
        body,
        out_shape=outs,
        in_specs=[smem() if kind == "s" else vmem() for kind in kinds],
        out_specs=jax.tree.map(lambda _: vmem(), outs),
        scratch_shapes=[pltpu.VMEM(shape, jnp.float32) for shape in scratch],
        name=body.__name__,
    )


def trade(value, axis, number):
    blocks = value.reshape(number, -1, 128)
    return lax.all_to_all(blocks, axis, split_axis=0, concat_axis=0, tiled=True).reshape(value.shape)


def local_step(orbitals, potential, unlocked):
    third, first, first_back, second, second_back = tables()
    outs = (f32(SLAB * 16, 128), f32(NB, ROWS, COLS, NG), f32(16, NG))
    made = call(forward_third, "svvv", outs, [(ROWS * 128, NG)])
    spectrum, local, sums = made(unlocked, orbitals.transpose(1, 2, 0, 3), potential, third)
    spectrum = trade(spectrum, "slab", SLAB)
    made = call(forward_first, "vv", f32(PENCIL * 16, 128), [(SLAB * 8, 128), (PENCIL * 8, 128)])
    spectrum = trade(made(spectrum, first), "pencil", PENCIL)
    scratch = [(PENCIL * 8, 128), (8 * 24, NG), (PENCIL * 8, 256), (PENCIL * 8, 128), (16, 128)]
    made = call(middle, "svvvv", f32(PENCIL * 8, 128), scratch)
    spectrum = trade(made(unlocked, spectrum, sums, second, second_back), "pencil", PENCIL)
    made = call(back_first, "vv", f32(SLAB * 8, 128), [(PENCIL * 8, 128), (SLAB * 8, 128)])
    spectrum = trade(made(spectrum, first_back), "slab", SLAB)
    made = call(back_third, "vvv", f32(ROWS, COLS, NB, NG), [(MODES, ROWS * HALF)])
    return made(spectrum, local, third).transpose(2, 0, 1, 3)


def solution(mesh):
    in_specs = (P(None, "slab", "pencil", None), P("slab", "pencil", None), P())
    out_specs = P(None, "slab", "pencil", None)
    return jax.shard_map(local_step, mesh=mesh, in_specs=in_specs, out_specs=out_specs, check_vma=False)
```

time: 102 us -> 90.4 us (0.89)
  blocking collectives: 58.5 us -> 77.1 us
  waiting for transfers between devices: 12.7 us -> 0 us
  starting transfers between devices: 12.4 us -> 0 us
  local copies, waits for them, and re-layouts: 4.35 us -> 0 us
    all_to_all x3 -> x4, blocking collectives: 58.5 us -> 77.1 us  [trade(): lax.all_to_all(blocks, axis, split_axis=0, concat_axis=0, tiled=True)]
    all_to_all x1 -> x0, waiting for transfers between devices: 12.7 us -> none  [local(): spectrum = three(unlocked, places, trade(spectrum, 'pencil'), sums)]
    all_to_all x1 -> x0, starting transfers between devices: 12.4 us -> none  [local(): spectrum = three(unlocked, places, trade(spectrum, 'pencil'), sums)]
    unnamed x3 -> x0, local copies, waits for them, and re-layouts: 2.45 us -> none
    pallas_call x1 -> x0, local copies, waits for them, and re-layouts: 1.9 us -> none  [five(): made(flags, orbitals, potential, given.reshape(SLAB * 16, 128), third_back)]
  transfers between devices with their start and end apart: 1 -> 0, of which waited for: 1 -> 0; matrix products, arithmetic and copies ran while one was open for 1% -> 0% of each run, Pallas kernels for 0% -> 0%
where the time goes in v2:
time: 90.4 us; the launch traced here: 90 us
  blocking collectives  77.1 us (85%)
  Pallas kernels  12.9 us (14%)
    all_to_all x4, blocking collectives, trade(): lax.all_to_all(blocks, axis, split_axis=0, concat_axis=0, tiled=True)  77.1 us
    pallas_call x1, Pallas kernels, local_step(): made(unlocked, spectrum, sums, second, second_back)  3.05 us
    pallas_call x1, Pallas kernels, local_step(): made(unlocked, orbitals.transpose(1, 2, 0, 3), potential, third)  2.89 us
    pallas_call x1, Pallas kernels, local_step(): return made(spectrum, local, third).transpose(2, 0, 1, 3)  2.59 us
    pallas_call x1, Pallas kernels, local_step(): spectrum = trade(made(spectrum, first), 'pencil', PENCIL)  2.2 us
    pallas_call x1, Pallas kernels, local_step(): spectrum = trade(made(spectrum, first_back), 'slab', SLAB)  2.11 us

profile of v2, /device:TPU:1, one launch (start us, length us, event | category | flops | bytes accessed | tf_op | source)
XLA Modules:
  0.0 90.0 jit_solution(9255204021046880528)
XLA Ops:
  0.0 2.9 %forward_third.1 = (f32[512,128]{1,0:T(8,128)}, f32[4,6,12,192]{3,2,1,0:T(8,128)}, f32[16,192]{1,0:T(8,128)}) custom-call(s32[4]{0:T(128)} %flags.3, f32[6,12,4,192]{3,2,1,0:T(4,128)} %bitcast.15, f32[6,12,192]{2,1,0:T(8,128)} %potential.1, f32[96,192]{1,0:T(8,128)} %constant.10.clone.table), custom_call_target="tpu_custom_call" | custom-call | tf_op jit(solution)/shard_map/forward_third/pallas_call | solution.py:251
  2.9 20.1 %all_to_all.20 = f32[32,16,128]{2,1,0:T(8,128)} all-to-all(f32[32,16,128]{2,1,0:T(8,128)} %bitcast.17), channel_id=1, replica_groups=mesh['slab'=32,'pencil'=16] {'slab'}, dimensions={0} | all-to-all | bytes 524288 | tf_op jit(solution)/shard_map/all_to_all | solution.py:244
  23.0 2.2 %forward_first.1 = f32[256,128]{1,0:T(8,128)} custom-call(f32[512,128]{1,0:T(8,128)} %bitcast.10, f32[128,256]{1,0:T(8,128)} %constant.11.clone.table), custom_call_target="tpu_custom_call" | custom-call | tf_op jit(solution)/shard_map/forward_first/pallas_call | solution.py:254
  25.2 24.7 %all_to_all.21 = f32[16,16,128]{2,1,0:T(8,128)} all-to-all(f32[16,16,128]{2,1,0:T(8,128)} %bitcast.14), channel_id=1, replica_groups=mesh['slab'=32,'pencil'=16] {'pencil'}, dimensions={0} | all-to-all | bytes 262144 | tf_op jit(solution)/shard_map/all_to_all | solution.py:244
  49.9 3.0 %middle.1 = f32[128,128]{1,0:T(8,128)} custom-call(s32[4]{0:T(128)} %flags.3, f32[256,128]{1,0:T(8,128)} %bitcast.13, f32[16,192]{1,0:T(8,128)} %get-tuple-element.9.sums, f32[192,128]{1,0:T(8,128)} %constant.12.clone.forward, f32[128,192]{1,0:T(8,128)} %constant.13.clone.back), custom_call_target="tpu_custom_call" | custom-call | tf_op jit(solution)/shard_map/middle/pallas_call | solution.py:257
  52.9 18.2 %all_to_all.22 = f32[16,8,128]{2,1,0:T(8,128)} all-to-all(f32[16,8,128]{2,1,0:T(8,128)} %bitcast.18), channel_id=1, replica_groups=mesh['slab'=32,'pencil'=16] {'pencil'}, dimensions={0} | all-to-all | bytes 131072 | tf_op jit(solution)/shard_map/all_to_all | solution.py:244
  71.1 2.1 %back_first.1 = f32[256,128]{1,0:T(8,128)} custom-call(f32[128,128]{1,0:T(8,128)} %bitcast.16, f32[256,128]{1,0:T(8,128)} %constant.14.clone.table), custom_call_target="tpu_custom_call" | custom-call | tf_op jit(solution)/shard_map/back_first/pallas_call | solution.py:259
  73.2 14.2 %all_to_all.23 = f32[32,8,128]{2,1,0:T(8,128)} all-to-all(f32[32,8,128]{2,1,0:T(8,128)} %bitcast.12), channel_id=1, replica_groups=mesh['slab'=32,'pencil'=16] {'slab'}, dimensions={0} | all-to-all | bytes 262144 | tf_op jit(solution)/shard_map/all_to_all | solution.py:244
  87.4 2.6 %back_third.1 = f32[6,12,4,192]{3,2,1,0:T(4,128)} custom-call(f32[256,128]{1,0:T(8,128)} %bitcast.11, f32[4,6,12,192]{3,2,1,0:T(8,128)} %get-tuple-element.10.local, f32[96,192]{1,0:T(8,128)} %constant.10.clone.table), custom_call_target="tpu_custom_call" | custom-call | tf_op jit(solution)/shard_map/back_third/pallas_call | solution.py:261

commit v3 on v2

--- a/solution.py
+++ b/solution.py
@@ -224,12 +224,16 @@
     return pl.BlockSpec(memory_space=pltpu.VMEM)
 
 
+def held(*shape):
+    return pltpu.VMEM(shape, jnp.float32)
+
+
 def f32(*shape):
     return jax.ShapeDtypeStruct(shape, jnp.float32)
 
 
 def call(body, kinds, outs, scratch=()):
-    return pl.pallas_call(
+    made = pl.pallas_call(
         body,
         out_shape=outs,
         in_specs=[smem() if kind == "s" else vmem() for kind in kinds],
@@ -238,6 +242,12 @@
         name=body.__name__,
     )
 
+    def run(*given):
+        kept = [pltpu.with_memory_space_constraint(x, pltpu.VMEM) if kind == "k" else x for kind, x in zip(kinds, given)]
+        return made(*kept)
+
+    return run
+
 
 def trade(value, axis, number):
     blocks = value.reshape(number, -1, 128)
@@ -246,18 +256,18 @@
 
 def local_step(orbitals, potential, unlocked):
     third, first, first_back, second, second_back = tables()
-    outs = (f32(SLAB * 16, 128), f32(NB, ROWS, COLS, NG), f32(16, NG))
+    outs = (held(SLAB * 16, 128), held(NB, ROWS, COLS, NG), held(16, NG))
     made = call(forward_third, "svvv", outs, [(ROWS * 128, NG)])
     spectrum, local, sums = made(unlocked, orbitals.transpose(1, 2, 0, 3), potential, third)
     spectrum = trade(spectrum, "slab", SLAB)
-    made = call(forward_first, "vv", f32(PENCIL * 16, 128), [(SLAB * 8, 128), (PENCIL * 8, 128)])
+    made = call(forward_first, "kv", held(PENCIL * 16, 128), [(SLAB * 8, 128), (PENCIL * 8, 128)])
     spectrum = trade(made(spectrum, first), "pencil", PENCIL)
     scratch = [(PENCIL * 8, 128), (8 * 24, NG), (PENCIL * 8, 256), (PENCIL * 8, 128), (16, 128)]
-    made = call(middle, "svvvv", f32(PENCIL * 8, 128), scratch)
+    made = call(middle, "skkvv", held(PENCIL * 8, 128), scratch)
     spectrum = trade(made(unlocked, spectrum, sums, second, second_back), "pencil", PENCIL)
-    made = call(back_first, "vv", f32(SLAB * 8, 128), [(PENCIL * 8, 128), (SLAB * 8, 128)])
+    made = call(back_first, "kv", held(SLAB * 8, 128), [(PENCIL * 8, 128), (SLAB * 8, 128)])
     spectrum = trade(made(spectrum, first_back), "slab", SLAB)
-    made = call(back_third, "vvv", f32(ROWS, COLS, NB, NG), [(MODES, ROWS * HALF)])
+    made = call(back_third, "kkv", f32(ROWS, COLS, NB, NG), [(MODES, ROWS * HALF)])
     return made(spectrum, local, third).transpose(2, 0, 1, 3)
 
 

time: 90.4 us -> 85.1 us (0.941)
  Pallas kernels: 12.9 us -> 9.82 us
  blocking collectives: 77.1 us -> 75 us
    pallas_call x5, Pallas kernels: 12.9 us -> 9.82 us  [run(): return made(*kept)]
    all_to_all x4, blocking collectives: 77.1 us -> 75 us  [trade(): lax.all_to_all(blocks, axis, split_axis=0, concat_axis=0, tiled=True)]
where the time goes in v3:
time: 85.1 us; the launch traced here: 84.8 us
  blocking collectives  75 us (88%)
  Pallas kernels  9.82 us (12%)
    all_to_all x4, blocking collectives, trade(): lax.all_to_all(blocks, axis, split_axis=0, concat_axis=0, tiled=True)  75 us
    pallas_call x5, Pallas kernels, run(): return made(*kept)  9.82 us

profile of v3, /device:TPU:1, one launch (start us, length us, event | category | flops | bytes accessed | tf_op | source)
XLA Modules:
  0.0 84.8 jit_solution(9743130665308776535)
XLA Ops:
  0.0 2.2 %forward_third.1 = (f32[512,128]{1,0:T(8,128)S(1)}, f32[4,6,12,192]{3,2,1,0:T(8,128)S(1)}, f32[16,192]{1,0:T(8,128)S(1)}) custom-call(s32[4]{0:T(128)} %flags.3, f32[6,12,4,192]{3,2,1,0:T(4,128)} %bitcast.18, f32[6,12,192]{2,1,0:T(8,128)} %potential.1, f32[96,192]{1,0:T(8,128)} %constant.10.clone.table), custom_call_target="tpu_custom_call" | custom-call | tf_op jit(solution)/shard_map/forward_third/pallas_call | solution.py:247
  2.2 18.5 %all_to_all.20 = f32[32,16,128]{2,1,0:T(8,128)S(1)} all-to-all(f32[32,16,128]{2,1,0:T(8,128)S(1)} %bitcast.16), channel_id=1, replica_groups=mesh['slab'=32,'pencil'=16] {'slab'}, dimensions={0} | all-to-all | bytes 524288 | tf_op jit(solution)/shard_map/all_to_all | solution.py:254
  20.8 1.5 %forward_first.1 = f32[256,128]{1,0:T(8,128)S(1)} custom-call(f32[512,128]{1,0:T(8,128)S(1)} %bitcast.10, f32[128,256]{1,0:T(8,128)} %constant.11.clone.table), custom_call_target="tpu_custom_call" | custom-call | tf_op jit(solution)/shard_map/forward_first/pallas_call | solution.py:247
  22.2 25.6 %all_to_all.21 = f32[16,16,128]{2,1,0:T(8,128)S(1)} all-to-all(f32[16,16,128]{2,1,0:T(8,128)S(1)} %bitcast.14), channel_id=1, replica_groups=mesh['slab'=32,'pencil'=16] {'pencil'}, dimensions={0} | all-to-all | bytes 262144 | tf_op jit(solution)/shard_map/all_to_all | solution.py:254
  47.8 2.3 %middle.1 = f32[128,128]{1,0:T(8,128)S(1)} custom-call(s32[4]{0:T(128)} %flags.3, f32[256,128]{1,0:T(8,128)S(1)} %bitcast.13, f32[16,192]{1,0:T(8,128)S(1)} %get-tuple-element.9.sums, f32[192,128]{1,0:T(8,128)} %constant.12.clone.forward, f32[128,192]{1,0:T(8,128)} %constant.13.clone.back), custom_call_target="tpu_custom_call" | custom-call | tf_op jit(solution)/shard_map/middle/pallas_call | solution.py:247
  50.2 17.9 %all_to_all.22 = f32[16,8,128]{2,1,0:T(8,128)S(1)} all-to-all(f32[16,8,128]{2,1,0:T(8,128)S(1)} %bitcast.17), channel_id=1, replica_groups=mesh['slab'=32,'pencil'=16] {'pencil'}, dimensions={0} | all-to-all | bytes 131072 | tf_op jit(solution)/shard_map/all_to_all | solution.py:254
  68.0 1.4 %back_first.1 = f32[256,128]{1,0:T(8,128)S(1)} custom-call(f32[128,128]{1,0:T(8,128)S(1)} %bitcast.15, f32[256,128]{1,0:T(8,128)} %constant.14.clone.table), custom_call_target="tpu_custom_call" | custom-call | tf_op jit(solution)/shard_map/back_first/pallas_call | solution.py:247
  69.4 12.9 %all_to_all.23 = f32[32,8,128]{2,1,0:T(8,128)S(1)} all-to-all(f32[32,8,128]{2,1,0:T(8,128)S(1)} %bitcast.12), channel_id=1, replica_groups=mesh['slab'=32,'pencil'=16] {'slab'}, dimensions={0} | all-to-all | bytes 262144 | tf_op jit(solution)/shard_map/all_to_all | solution.py:254
  82.4 2.4 %back_third.1 = f32[6,12,4,192]{3,2,1,0:T(4,128)} custom-call(f32[256,128]{1,0:T(8,128)S(1)} %bitcast.11, f32[4,6,12,192]{3,2,1,0:T(8,128)S(1)} %get-tuple-element.10.local, f32[96,192]{1,0:T(8,128)} %constant.10.clone.table), custom_call_target="tpu_custom_call" | custom-call | tf_op jit(solution)/shard_map/back_third/pallas_call | solution.py:247

commit v4 on v3

--- a/solution.py
+++ b/solution.py
@@ -260,14 +260,14 @@
     made = call(forward_third, "svvv", outs, [(ROWS * 128, NG)])
     spectrum, local, sums = made(unlocked, orbitals.transpose(1, 2, 0, 3), potential, third)
     spectrum = trade(spectrum, "slab", SLAB)
-    made = call(forward_first, "kv", held(PENCIL * 16, 128), [(SLAB * 8, 128), (PENCIL * 8, 128)])
+    made = call(forward_first, "kk", held(PENCIL * 16, 128), [(SLAB * 8, 128), (PENCIL * 8, 128)])
     spectrum = trade(made(spectrum, first), "pencil", PENCIL)
     scratch = [(PENCIL * 8, 128), (8 * 24, NG), (PENCIL * 8, 256), (PENCIL * 8, 128), (16, 128)]
-    made = call(middle, "skkvv", held(PENCIL * 8, 128), scratch)
+    made = call(middle, "skkkk", held(PENCIL * 8, 128), scratch)
     spectrum = trade(made(unlocked, spectrum, sums, second, second_back), "pencil", PENCIL)
-    made = call(back_first, "kv", held(SLAB * 8, 128), [(PENCIL * 8, 128), (SLAB * 8, 128)])
+    made = call(back_first, "kk", held(SLAB * 8, 128), [(PENCIL * 8, 128), (SLAB * 8, 128)])
     spectrum = trade(made(spectrum, first_back), "slab", SLAB)
-    made = call(back_third, "kkv", f32(ROWS, COLS, NB, NG), [(MODES, ROWS * HALF)])
+    made = call(back_third, "kkk", f32(ROWS, COLS, NB, NG), [(MODES, ROWS * HALF)])
     return made(spectrum, local, third).transpose(2, 0, 1, 3)
 
 

time: 85.1 us -> 82.7 us (0.972)
  Pallas kernels: 9.82 us -> 6.83 us
    pallas_call x5, Pallas kernels: 9.82 us -> 6.83 us  [run(): return made(*kept)]
where the time goes in v4:
time: 82.7 us; the launch traced here: 82.4 us
  blocking collectives  75.5 us (91%)
  Pallas kernels  6.83 us (8%)
    all_to_all x4, blocking collectives, trade(): lax.all_to_all(blocks, axis, split_axis=0, concat_axis=0, tiled=True)  75.5 us
    pallas_call x5, Pallas kernels, run(): return made(*kept)  6.83 us

profile of v4, /device:TPU:1, one launch (start us, length us, event | category | flops | bytes accessed | tf_op | source)
XLA Modules:
  0.0 82.4 jit_solution(2449229113160709967)
XLA Ops:
  0.0 2.2 %forward_third.1 = (f32[512,128]{1,0:T(8,128)S(1)}, f32[4,6,12,192]{3,2,1,0:T(8,128)S(1)}, f32[16,192]{1,0:T(8,128)S(1)}) custom-call(s32[4]{0:T(128)} %flags.3, f32[6,12,4,192]{3,2,1,0:T(4,128)} %bitcast.18, f32[6,12,192]{2,1,0:T(8,128)} %potential.1, f32[96,192]{1,0:T(8,128)} %constant.10.clone.table), custom_call_target="tpu_custom_call" | custom-call | tf_op jit(solution)/shard_map/forward_third/pallas_call | solution.py:247
  2.2 0.0 copy-start.3
  2.2 18.7 %all_to_all.20 = f32[32,16,128]{2,1,0:T(8,128)S(1)} all-to-all(f32[32,16,128]{2,1,0:T(8,128)S(1)} %bitcast.16), channel_id=1, replica_groups=mesh['slab'=32,'pencil'=16] {'slab'}, dimensions={0} | all-to-all | bytes 524288 | tf_op jit(solution)/shard_map/all_to_all | solution.py:254
  20.9 0.0 copy-done.3
  20.9 0.6 forward_first.1
  21.5 0.0 copy-start.2
  21.5 0.0 copy-start.4
  21.5 25.8 %all_to_all.21 = f32[16,16,128]{2,1,0:T(8,128)S(1)} all-to-all(f32[16,16,128]{2,1,0:T(8,128)S(1)} %bitcast.14), channel_id=1, replica_groups=mesh['slab'=32,'pencil'=16] {'pencil'}, dimensions={0} | all-to-all | bytes 262144 | tf_op jit(solution)/shard_map/all_to_all | solution.py:254
  47.2 0.0 copy-done.2
  47.2 0.0 copy-done.4
  47.3 2.0 %middle.1 = f32[128,128]{1,0:T(8,128)S(1)} custom-call(s32[4]{0:T(128)} %flags.3, f32[256,128]{1,0:T(8,128)S(1)} %bitcast.13, f32[16,192]{1,0:T(8,128)S(1)} %get-tuple-element.9.sums, f32[192,128]{1,0:T(8,128)S(1)} %copy-done.4, f32[128,192]{1,0:T(8,128)S(1)} %copy-done.2), custom_call_target="tpu_custom_call" | custom-call | tf_op jit(solution)/shard_map/middle/pallas_call | solution.py:247
  49.3 0.0 copy-start.1
  49.3 18.0 %all_to_all.22 = f32[16,8,128]{2,1,0:T(8,128)S(1)} all-to-all(f32[16,8,128]{2,1,0:T(8,128)S(1)} %bitcast.17), channel_id=1, replica_groups=mesh['slab'=32,'pencil'=16] {'pencil'}, dimensions={0} | all-to-all | bytes 131072 | tf_op jit(solution)/shard_map/all_to_all | solution.py:254
  67.3 0.0 copy-done.1
  67.3 0.5 back_first.1
  67.8 0.0 copy-start
  67.8 13.1 %all_to_all.23 = f32[32,8,128]{2,1,0:T(8,128)S(1)} all-to-all(f32[32,8,128]{2,1,0:T(8,128)S(1)} %bitcast.12), channel_id=1, replica_groups=mesh['slab'=32,'pencil'=16] {'slab'}, dimensions={0} | all-to-all | bytes 262144 | tf_op jit(solution)/shard_map/all_to_all | solution.py:254
  80.9 0.0 copy-done
  80.9 1.5 %back_third.1 = f32[6,12,4,192]{3,2,1,0:T(4,128)} custom-call(f32[256,128]{1,0:T(8,128)S(1)} %bitcast.11, f32[4,6,12,192]{3,2,1,0:T(8,128)S(1)} %get-tuple-element.10.local, f32[96,192]{1,0:T(8,128)S(1)} %copy-done), custom_call_target="tpu_custom_call" | custom-call | tf_op jit(solution)/shard_map/back_third/pallas_call | solution.py:247
Async XLA Ops:
  2.2 18.7 %copy-start.3 = (f32[128,256]{1,0:T(8,128)S(1)}, f32[128,256]{1,0:T(8,128)}, u32[]{:S(2)}) copy-start(f32[128,256]{1,0:T(8,128)} %constant.11.clone.table) | copy-start | bytes 393220
  21.5 25.8 %copy-start.2 = (f32[128,192]{1,0:T(8,128)S(1)}, f32[128,192]{1,0:T(8,128)}, u32[]{:S(2)}) copy-start(f32[128,192]{1,0:T(8,128)} %constant.13.clone.back) | copy-start | bytes 294916
  21.5 25.8 %copy-start.4 = (f32[192,128]{1,0:T(8,128)S(1)}, f32[192,128]{1,0:T(8,128)}, u32[]{:S(2)}) copy-start(f32[192,128]{1,0:T(8,128)} %constant.12.clone.forward) | copy-start | bytes 294916
  49.3 18.0 %copy-start.1 = (f32[256,128]{1,0:T(8,128)S(1)}, f32[256,128]{1,0:T(8,128)}, u32[]{:S(2)}) copy-start(f32[256,128]{1,0:T(8,128)} %constant.14.clone.table) | copy-start | bytes 393220
  67.8 13.1 %copy-start = (f32[96,192]{1,0:T(8,128)S(1)}, f32[96,192]{1,0:T(8,128)}, u32[]{:S(2)}) copy-start(f32[96,192]{1,0:T(8,128)} %constant.10.clone.table) | copy-start | bytes 221188

commit v5 on v4

--- a/solution.py
+++ b/solution.py
@@ -38,8 +38,9 @@
     first = np.zeros((PENCIL, 8, SLAB, 8))
     first[:, :FIRSTS, :, :ROWS] = real.reshape(PENCIL, FIRSTS, SLAB, ROWS)
     first = first.reshape(PENCIL * 8, SLAB * 8)
-    second = np.zeros((128, NG))
-    second[:MODES] = real
+    second = np.zeros((128, 2, 128))
+    second[:MODES, :, : NG // 2] = real.reshape(MODES, 2, NG // 2)
+    second = second.reshape(128, 256)
     made = (third, first, first.T, second.T, second)
     return [np.ascontiguousarray(t, dtype=np.float32) for t in made]
 
@@ -68,6 +69,8 @@
 
 def forward_third(flags, orbitals, potential, table, out, local, sums, lines):
     totals = [None] * len(PAIRS)
+    whole = lanes(SLAB, 128)
+    last = []
     for i in range(ROWS):
         shifted = (potential[i] - 1.0) * (1.0 / 1.5)
         own = []
@@ -75,7 +78,7 @@
             base = i * 128 + b * COLS
             value = orbitals[i, :, b, :]
             kept = jnp.where(flags[b] == 1, value * shifted, value)
-            lines[base : base + COLS, :] = value
+            lines[base : base + COLS, :] = value * jnp.where(flags[b] == 1, 1.0 / 1.5, 0.0)
             lines[base + HALF : base + HALF + COLS, :] = kept
             local[b, i] = kept
             own.append(kept)
@@ -85,15 +88,15 @@
     sums[...] = jnp.zeros_like(sums)
     for q in range(len(PAIRS)):
         sums[q : q + 1, :] = jnp.sum(totals[q], axis=0, keepdims=True)
-    spectrum = dot(table[...], lines[...], ((1,), (1,)))
-    whole = lanes(SLAB, 128)
-    last = []
-    for i in range(ROWS):
-        parts = [spectrum[t * 32 : t * 32 + 32, i * 128 : i * 128 + 128] for t in range(THIRDS)]
-        for t in range(2):
-            extra = turn(parts[2], WIDE - 32 * t)
-            out[pl.ds(t * 8 + i, SLAB, stride=16), :] = jnp.where(whole < WIDE, parts[t], extra)
-        last.append(parts[2])
+    for pair in range(ROWS // 2):
+        spectrum = dot(table[...], lines[pair * 256 : pair * 256 + 256, :], ((1,), (1,)))
+        for i in (2 * pair, 2 * pair + 1):
+            at = i % 2 * 128
+            parts = [spectrum[t * 32 : t * 32 + 32, at : at + 128] for t in range(THIRDS)]
+            for t in range(2):
+                extra = turn(parts[2], WIDE - 32 * t)
+                out[pl.ds(t * 8 + i, SLAB, stride=16), :] = jnp.where(whole < WIDE, parts[t], extra)
+            last.append(parts[2])
     for t in range(2):
         out[pl.ds(t * 8 + 6, SLAB, stride=16), :] = gathered(last[t * 4 : t * 4 + 4], 32, 64)
         out[pl.ds(t * 8 + 7, SLAB, stride=16), :] = jnp.zeros((SLAB, 128), jnp.float32)
@@ -116,20 +119,28 @@
         out[pl.ds(t * 8 + 6, PENCIL, stride=16), :] = gathered(pieces[t * 4 : t * 4 + 4], 32, 0)
 
 
-def middle(flags, given, sums, forward, back, out, third, lines, wide, more, rows):
+def middle(given, sums, forward, back, out, third, lines, more, rows):
     rest = [given[pl.ds(t * 8 + 6, PENCIL, stride=16), :] for t in range(2)]
     for i in range(8):
         value = turn(rest[i // 4], 64 - 32 * (i % 4)) if i < FIRSTS else jnp.zeros((PENCIL, 128), jnp.float32)
         third[pl.ds(i, PENCIL, stride=8), :] = value
     lane = lanes(8, 128)
-    for p in range(PENCIL):
-        parts = [given[p * 16 : p * 16 + 8, :], given[p * 16 + 8 : p * 16 + 16, :]]
-        last = jnp.where(lane < 64, turn(parts[1], 64), third[p * 8 : p * 8 + 8, :])
-        parts.append(jnp.where(lane < 32, turn(parts[0], 32), last))
-        for u in range(2 * NB):
+    masks = [((lane - COLS * m) & 127) < COLS for m in range(17)]
+    for h in range(2):
+        turned = [[], [], []]
+        for k in range(8):
+            p = 8 * h + k
+            parts = [given[p * 16 : p * 16 + 8, :], given[p * 16 + 8 : p * 16 + 16, :]]
+            last = jnp.where(lane < 64, turn(parts[1], 64), third[p * 8 : p * 8 + 8, :])
+            parts.append(jnp.where(lane < 32, turn(parts[0], 32), last))
             for t in range(THIRDS):
-                at = u * 24 + t * 8
-                lines[at : at + 8, p * COLS : p * COLS + COLS] = parts[t][:, u * COLS : u * COLS + COLS]
+                turned[t].append(turn(parts[t], COLS * k))
+        for t in range(THIRDS):
+            for u in range(2 * NB):
+                value = turned[t][0]
+                for k in range(1, 8):
+                    value = jnp.where(masks[k + u], turned[t][k], value)
+                lines[u * 24 + t * 8 : u * 24 + t * 8 + 8, h * 128 : h * 128 + 128] = turn(value, -COLS * u)
     spectrum = dot(lines[...], forward[...])
     row = lax.broadcasted_iota(jnp.int32, (24, 128), 0)
     lane = lanes(24, 128)
@@ -147,8 +158,7 @@
     weight = weight * kinetic
     scaled, other = [], []
     for b in range(NB):
-        alpha = jnp.where(flags[b] == 1, 1.0 / 1.5, 0.0)
-        value = spectrum[b * 24 : b * 24 + 24] * alpha
+        value = spectrum[b * 24 : b * 24 + 24]
         scaled.append(value * weight)
         other.append(0.5 * kinetic * value + spectrum[(NB + b) * 24 : (NB + b) * 24 + 24])
     returned = dot(jnp.concatenate(scaled, axis=0), back[...])
@@ -157,47 +167,53 @@
         term = scaled[a] * other[b] + scaled[b] * other[a]
         rows[q : q + 1, :] = jnp.sum(term[:8] + term[8:16] + term[16:], axis=0, keepdims=True)
     total = jnp.sum(rows[...], axis=1, keepdims=True) + jnp.sum(sums[...], axis=1, keepdims=True)
-    picked = lax.broadcasted_iota(jnp.int32, (16, 128), 0) == lanes(16, 128)
+    picked = lax.broadcasted_iota(jnp.int32, (16, 128), 0) + 64 == lanes(16, 128)
     note = jnp.sum(jnp.where(picked, total, 0.0), axis=0, keepdims=True)
-    for p in range(PENCIL):
-        for b in range(NB):
-            for t in range(THIRDS):
-                at = t * HALF + b * COLS
-                wide[p * 8 : p * 8 + 8, at : at + COLS] = returned[b * 24 + t * 8 : b * 24 + t * 8 + 8, p * COLS : p * COLS + COLS]
-    more[...] = wide[:, 128:256]
-    out[...] = wide[:, 0:128]
+    for h in range(2):
+        turned = []
+        for c in range(NB * THIRDS):
+            t, b = c // NB, c % NB
+            value = returned[b * 24 + t * 8 : b * 24 + t * 8 + 8, h * 128 : h * 128 + 128]
+            turned.append(turn(value, COLS * (c if c < 10 else c - 10)))
+        for k in range(8):
+            p = 8 * h + k
+            value = turned[0]
+            for c in range(1, 10):
+                value = jnp.where(masks[k + c], turned[c], value)
+            out[p * 8 : p * 8 + 8, :] = turn(value, -COLS * k)
+            more[p * 8 : p * 8 + 8, :] = turn(jnp.where(masks[k + 1], turned[11], turned[10]), -COLS * k)
     pieces = [more[pl.ds(i, PENCIL, stride=8), :] for i in range(FIRSTS)]
-    out[pl.ds(6, PENCIL, stride=8), :] = gathered(pieces, 16, 0)
-    out[pl.ds(7, PENCIL, stride=8), :] = jnp.broadcast_to(note, (PENCIL, 128))
+    out[pl.ds(6, PENCIL, stride=8), :] = gathered(pieces[:5], 24, 0)
+    out[pl.ds(7, PENCIL, stride=8), :] = jnp.where(lanes(PENCIL, 128) < 24, pieces[5], note)
 
 
 def back_first(given, table, out, taken, made):
-    rest = given[pl.ds(6, PENCIL, stride=8), :]
+    rest = [given[pl.ds(i, PENCIL, stride=8), :] for i in (6, 7)]
     for i in range(8):
-        value = turn(rest, -16 * i) if i < FIRSTS else jnp.zeros((PENCIL, 128), jnp.float32)
+        value = turn(rest[i // 5], -24 * (i % 5)) if i < FIRSTS else jnp.zeros((PENCIL, 128), jnp.float32)
         taken[pl.ds(i, PENCIL, stride=8), :] = value
     out[...] = dot(table[...], given[...])
     made[...] = dot(table[...], taken[...])
     pieces = [made[pl.ds(i, SLAB, stride=8), :] for i in range(ROWS)]
-    out[pl.ds(6, SLAB, stride=8), :] = gathered(pieces, 16, 0)
-    note = jnp.sum(given[pl.ds(7, PENCIL, stride=8), :], axis=0, keepdims=True)
-    out[pl.ds(7, SLAB, stride=8), :] = jnp.broadcast_to(note, (SLAB, 128))
+    out[pl.ds(6, SLAB, stride=8), :] = gathered(pieces[:5], 24, 0)
+    note = jnp.sum(rest[1], axis=0, keepdims=True)
+    out[pl.ds(7, SLAB, stride=8), :] = jnp.where(lanes(SLAB, 128) < 24, pieces[5], note)
 
 
 def back_third(given, local, table, out, lines):
-    rest = given[pl.ds(6, SLAB, stride=8), :]
+    rest = [given[pl.ds(i, SLAB, stride=8), :] for i in (6, 7)]
     for i in range(ROWS):
         value = given[pl.ds(i, SLAB, stride=8), :]
         at = i * HALF
         lines[0:32, at : at + HALF] = value[:, :HALF]
         lines[32:64, at : at + HALF] = value[:, HALF:WIDE]
-        lines[64:96, at : at + 32] = value[:, WIDE:128]
-        lines[64:96, at + 32 : at + HALF] = rest[:, 16 * i : 16 * i + 16]
+        lines[64:96, at : at + 24] = value[:, WIDE : WIDE + 24]
+        lines[64:96, at + 24 : at + HALF] = rest[i // 5][:, 24 * (i % 5) : 24 * (i % 5) + 24]
     kinetic_part = dot(lines[...], table[...], ((0,), (0,)))
-    note = jnp.sum(given[pl.ds(7, SLAB, stride=8), :], axis=0, keepdims=True) * (1.0 / CELLS)
+    note = jnp.sum(rest[1], axis=0, keepdims=True) * (1.0 / CELLS)
     factor, inverse = {}, {}
     for q, (a, b) in enumerate(PAIRS):
-        value = note[:, q : q + 1]
+        value = note[:, 64 + q : 65 + q]
         for c in range(b):
             value = value - factor[a, c] * factor[b, c]
         if a == b:
@@ -262,9 +278,9 @@
     spectrum = trade(spectrum, "slab", SLAB)
     made = call(forward_first, "kk", held(PENCIL * 16, 128), [(SLAB * 8, 128), (PENCIL * 8, 128)])
     spectrum = trade(made(spectrum, first), "pencil", PENCIL)
-    scratch = [(PENCIL * 8, 128), (8 * 24, NG), (PENCIL * 8, 256), (PENCIL * 8, 128), (16, 128)]
-    made = call(middle, "skkkk", held(PENCIL * 8, 128), scratch)
-    spectrum = trade(made(unlocked, spectrum, sums, second, second_back), "pencil", PENCIL)
+    scratch = [(PENCIL * 8, 128), (8 * 24, 256), (PENCIL * 8, 128), (16, 128)]
+    made = call(middle, "kkkk", held(PENCIL * 8, 128), scratch)
+    spectrum = trade(made(spectrum, sums, second, second_back), "pencil", PENCIL)
     made = call(back_first, "kk", held(SLAB * 8, 128), [(PENCIL * 8, 128), (SLAB * 8, 128)])
     spectrum = trade(made(spectrum, first_back), "slab", SLAB)
     made = call(back_third, "kkk", f32(ROWS, COLS, NB, NG), [(MODES, ROWS * HALF)])

time: 82.7 us -> 81.9 us (level)
  no operation moved by 1% of the time
where the time goes in v5:
time: 81.9 us; the launch traced here: 81.6 us
  blocking collectives  75.5 us (92%)
  Pallas kernels  6.02 us (7%)
    all_to_all x4, blocking collectives, trade(): lax.all_to_all(blocks, axis, split_axis=0, concat_axis=0, tiled=True)  75.5 us
    pallas_call x5, Pallas kernels, run(): return made(*kept)  6.02 us

profile of v5, /device:TPU:1, one launch (start us, length us, event | category | flops | bytes accessed | tf_op | source)
XLA Modules:
  0.0 81.6 jit_solution(1395827775716901741)
XLA Ops:
  0.0 2.3 %forward_third.1 = (f32[512,128]{1,0:T(8,128)S(1)}, f32[4,6,12,192]{3,2,1,0:T(8,128)S(1)}, f32[16,192]{1,0:T(8,128)S(1)}) custom-call(s32[4]{0:T(128)} %flags.1, f32[6,12,4,192]{3,2,1,0:T(4,128)} %bitcast.18, f32[6,12,192]{2,1,0:T(8,128)} %potential.1, f32[96,192]{1,0:T(8,128)} %constant.10.clone.table), custom_call_target="tpu_custom_call" | custom-call | tf_op jit(solution)/shard_map/forward_third/pallas_call | solution.py:263
  2.3 0.0 copy-start.4
  2.4 18.7 %all_to_all.20 = f32[32,16,128]{2,1,0:T(8,128)S(1)} all-to-all(f32[32,16,128]{2,1,0:T(8,128)S(1)} %bitcast.16), channel_id=1, replica_groups=mesh['slab'=32,'pencil'=16] {'slab'}, dimensions={0} | all-to-all | bytes 524288 | tf_op jit(solution)/shard_map/all_to_all | solution.py:270
  21.0 0.0 copy-done.4
  21.0 0.6 forward_first.1
  21.6 0.0 copy-start.2
  21.6 0.0 copy-start.3
  21.6 25.8 %all_to_all.21 = f32[16,16,128]{2,1,0:T(8,128)S(1)} all-to-all(f32[16,16,128]{2,1,0:T(8,128)S(1)} %bitcast.14), channel_id=1, replica_groups=mesh['slab'=32,'pencil'=16] {'pencil'}, dimensions={0} | all-to-all | bytes 262144 | tf_op jit(solution)/shard_map/all_to_all | solution.py:270
  47.4 0.0 copy-done.2
  47.4 0.0 copy-done.3
  47.4 1.1 %middle.1 = f32[128,128]{1,0:T(8,128)S(1)} custom-call(f32[256,128]{1,0:T(8,128)S(1)} %bitcast.13, f32[16,192]{1,0:T(8,128)S(1)} %get-tuple-element.9.sums, f32[256,128]{1,0:T(8,128)S(1)} %copy-done.3, f32[128,256]{1,0:T(8,128)S(1)} %copy-done.2), custom_call_target="tpu_custom_call" | custom-call | tf_op jit(solution)/shard_map/middle/pallas_call | solution.py:263
  48.5 0.0 copy-start.1
  48.5 18.0 %all_to_all.22 = f32[16,8,128]{2,1,0:T(8,128)S(1)} all-to-all(f32[16,8,128]{2,1,0:T(8,128)S(1)} %bitcast.17), channel_id=1, replica_groups=mesh['slab'=32,'pencil'=16] {'pencil'}, dimensions={0} | all-to-all | bytes 131072 | tf_op jit(solution)/shard_map/all_to_all | solution.py:270
  66.5 0.0 copy-done.1
  66.5 0.5 back_first.1
  67.0 0.0 copy-start
  67.0 13.1 %all_to_all.23 = f32[32,8,128]{2,1,0:T(8,128)S(1)} all-to-all(f32[32,8,128]{2,1,0:T(8,128)S(1)} %bitcast.12), channel_id=1, replica_groups=mesh['slab'=32,'pencil'=16] {'slab'}, dimensions={0} | all-to-all | bytes 262144 | tf_op jit(solution)/shard_map/all_to_all | solution.py:270
  80.1 0.0 copy-done
  80.1 1.5 %back_third.1 = f32[6,12,4,192]{3,2,1,0:T(4,128)} custom-call(f32[256,128]{1,0:T(8,128)S(1)} %bitcast.11, f32[4,6,12,192]{3,2,1,0:T(8,128)S(1)} %get-tuple-element.10.local, f32[96,192]{1,0:T(8,128)S(1)} %copy-done), custom_call_target="tpu_custom_call" | custom-call | tf_op jit(solution)/shard_map/back_third/pallas_call | solution.py:263
Async XLA Ops:
  2.3 18.7 %copy-start.4 = (f32[128,256]{1,0:T(8,128)S(1)}, f32[128,256]{1,0:T(8,128)}, u32[]{:S(2)}) copy-start(f32[128,256]{1,0:T(8,128)} %constant.11.clone.table) | copy-start | bytes 393220
  21.6 25.8 %copy-start.2 = (f32[128,256]{1,0:T(8,128)S(1)}, f32[128,256]{1,0:T(8,128)}, u32[]{:S(2)}) copy-start(f32[128,256]{1,0:T(8,128)} %constant.13.clone.back) | copy-start | bytes 393220
  21.6 25.8 %copy-start.3 = (f32[256,128]{1,0:T(8,128)S(1)}, f32[256,128]{1,0:T(8,128)}, u32[]{:S(2)}) copy-start(f32[256,128]{1,0:T(8,128)} %constant.12.clone.forward) | copy-start | bytes 393220
  48.5 18.0 %copy-start.1 = (f32[256,128]{1,0:T(8,128)S(1)}, f32[256,128]{1,0:T(8,128)}, u32[]{:S(2)}) copy-start(f32[256,128]{1,0:T(8,128)} %constant.14.clone.table) | copy-start | bytes 393220
  67.0 13.1 %copy-start = (f32[96,192]{1,0:T(8,128)S(1)}, f32[96,192]{1,0:T(8,128)}, u32[]{:S(2)}) copy-start(f32[96,192]{1,0:T(8,128)} %constant.10.clone.table) | copy-start | bytes 221188

commit v6 on v5

v6 whole, which is shorter than its diff:
```python
import functools

import jax
import jax.numpy as jnp
import numpy as np
from jax import lax
from jax.experimental import pallas as pl
from jax.experimental.pallas import tpu as pltpu
from jax.sharding import PartitionSpec as P

NG = 192
NB = 4
CUT = NG // 4
MODES = 2 * CUT
SLAB = 32
PENCIL = 16
ROWS = NG // SLAB
COLS = NG // PENCIL
CELLS = float(NG**3)
THIRDS = MODES // SLAB
FIRSTS = MODES // PENCIL
WIDE = 2 * NB * COLS
HALF = NB * COLS
PAIRS = [(a, b) for a in range(NB) for b in range(a + 1)]
highest = lax.Precision.HIGHEST


def basis():
    place = np.arange(NG)
    mode = np.arange(MODES)
    angle = 2.0 * np.pi / NG * ((mode[:, None] % CUT) * place[None, :] % NG)
    return np.where(mode[:, None] < CUT, np.cos(angle), np.sin(angle))


def tables():
    real = basis()
    third = real.reshape(SLAB, THIRDS, NG).transpose(1, 0, 2).reshape(MODES, NG)
    first = real.reshape(PENCIL, FIRSTS, SLAB, ROWS).transpose(1, 0, 3, 2).reshape(MODES, NG)
    second = np.zeros((128, 2, 128))
    second[:MODES, :, : NG // 2] = real.reshape(MODES, 2, NG // 2)
    second = second.reshape(128, 256)
    made = (third, first, first.T, second.T, second)
    return [np.ascontiguousarray(t, dtype=np.float32) for t in made]


def dot(a, b, dims=((1,), (0,))):
    return lax.dot_general(a, b, (dims, ((), ())), precision=highest, preferred_element_type=jnp.float32)


def lanes(*shape):
    return lax.broadcasted_iota(jnp.int32, shape, len(shape) - 1)


def turn(value, by):
    by = by % 128
    return pltpu.roll(value, by, 1) if by else value


def gathered(pieces, width, start):
    lane = lanes(*pieces[0].shape)
    result = jnp.zeros(pieces[0].shape, jnp.float32)
    for k, piece in enumerate(pieces):
        here = (lane >= k * width) & (lane < k * width + width)
        result = jnp.where(here, turn(piece, k * width - start), result)
    return result


def forward_third(flags, orbitals, potential, table, out, local, sums, kind, low, high, field, made, lines, ready):
    copies = [pltpu.make_async_copy(flags, kind, ready.at[0]), pltpu.make_async_copy(potential, field, ready.at[1])]
    copies += [pltpu.make_async_copy(orbitals.at[i, :, :, 0:128], low.at[i], ready.at[2 + i]) for i in range(ROWS)]
    copies += [pltpu.make_async_copy(orbitals.at[i, :, :, 128:NG], high.at[i], ready.at[2 + ROWS + i]) for i in range(ROWS)]
    copies.append(pltpu.make_async_copy(table, made, ready.at[2 + 2 * ROWS]))
    low, high = low.reshape(ROWS * COLS * NB, 128), high.reshape(ROWS * COLS * NB, 64)
    for copy in copies:
        copy.start()
    copies[0].wait()
    copies[1].wait()
    totals = [None] * len(PAIRS)
    for i in range(ROWS):
        copies[2 + i].wait()
        copies[2 + ROWS + i].wait()
        shifted = (field[i] - 1.0) * (1.0 / 1.5)
        own = []
        for b in range(NB):
            base = i * WIDE + b * COLS
            parts = [ref[pl.ds(i * WIDE // 2 + b, COLS, stride=NB), :] for ref in (low, high)]
            value = jnp.concatenate([parts[0], parts[1]], axis=1)
            kept = jnp.where(kind[b] == 1, value * shifted, value)
            lines[base : base + COLS, :] = value * jnp.where(kind[b] == 1, 1.0 / 1.5, 0.0)
            lines[base + HALF : base + HALF + COLS, :] = kept
            local[b, i] = kept
            own.append(kept)
        for q, (a, b) in enumerate(PAIRS):
            term = own[a] * own[b]
            totals[q] = term if totals[q] is None else totals[q] + term
    copies[-1].wait()
    whole = lanes(SLAB, 128)
    last = []
    for i in range(ROWS):
        if i % 2 == 0:
            spectrum = dot(made[...], lines[i * WIDE : i * WIDE + 2 * WIDE, :], ((1,), (1,)))
            result = spectrum[:, :128]
        else:
            more = jnp.concatenate([spectrum[:, 128:], jnp.zeros((MODES, 64), jnp.float32)], axis=1)
            result = jnp.where(lanes(MODES, 128) < 32, turn(spectrum[:, :128], 32), turn(more, 32))
        parts = [result[t * 32 : t * 32 + 32] for t in range(THIRDS)]
        for t in range(2):
            extra = turn(parts[2], WIDE - 32 * t)
            out[pl.ds(t * 7 + i, SLAB, stride=14), :] = jnp.where(whole < WIDE, parts[t], extra)
        last.append(parts[2])
    sums[...] = jnp.zeros_like(sums)
    for q in range(len(PAIRS)):
        sums[q : q + 1, :] = jnp.sum(totals[q], axis=0, keepdims=True)
    for t in range(2):
        out[pl.ds(t * 7 + 6, SLAB, stride=14), :] = gathered(last[t * 4 : t * 4 + 4], 32, 64)


def forward_first(given, table, out):
    for t in range(2):
        block = jnp.concatenate([given[pl.ds(t * 7 + i, SLAB, stride=14), :] for i in range(ROWS)], axis=0)
        result = dot(table[...], block)
        for i in range(FIRSTS):
            out[pl.ds(t * 7 + i, PENCIL, stride=14), :] = result[i * PENCIL : (i + 1) * PENCIL]
    rest = [given[pl.ds(t * 7 + 6, SLAB, stride=14), :] for t in range(2)]
    block = jnp.concatenate([turn(rest[i // 4], -32 * (i % 4)) for i in range(ROWS)], axis=0)
    result = dot(table[...], block)
    pieces = [result[i * PENCIL : (i + 1) * PENCIL] for i in range(FIRSTS)]
    for t in range(2):
        out[pl.ds(t * 7 + 6, PENCIL, stride=14), :] = gathered(pieces[t * 4 : t * 4 + 4], 32, 0)


def middle(given, sums, forward, back, out, tiles, lines, more, rows):
    rest = [given[pl.ds(t * 7 + 6, PENCIL, stride=14), :] for t in range(2)]
    lane = lanes(PENCIL, 128)
    empty = jnp.zeros((PENCIL, 128), jnp.float32)
    for i in range(8):
        parts = [empty] * THIRDS
        if i < FIRSTS:
            parts = [given[pl.ds(t * 7 + i, PENCIL, stride=14), :] for t in range(2)]
            last = jnp.where(lane < 64, turn(parts[1], 64), turn(rest[i // 4], 64 - 32 * (i % 4)))
            parts.append(jnp.where(lane < 32, turn(parts[0], 32), last))
        for t in range(THIRDS):
            tiles[pl.ds(t * 128 + i, PENCIL, stride=8), :] = parts[t]
    lane = lanes(8, 128)
    masks = [((lane - COLS * m) & 127) < COLS for m in range(17)]
    for h in range(2):
        for t in range(THIRDS):
            turned = []
            for k in range(8):
                at = t * 128 + (8 * h + k) * 8
                turned.append(turn(tiles[at : at + 8, :], COLS * k))
            for u in range(2 * NB):
                value = turned[0]
                for k in range(1, 8):
                    value = jnp.where(masks[k + u], turned[k], value)
                lines[u * 24 + t * 8 : u * 24 + t * 8 + 8, h * 128 : h * 128 + 128] = turn(value, -COLS * u)
    spectrum = dot(lines[...], forward[...])
    row = lax.broadcasted_iota(jnp.int32, (24, 128), 0)
    lane = lanes(24, 128)
    third_mode = THIRDS * lax.axis_index("slab") + row // 8
    first_mode = FIRSTS * lax.axis_index("pencil") + row % 8
    known = (row % 8 < FIRSTS) & (lane < MODES)
    squared = jnp.zeros((24, 128), jnp.int32)
    weight = jnp.full((24, 128), 1.0 / CELLS, jnp.float32)
    for mode in (third_mode, first_mode, lane):
        size = jnp.where(mode < CUT, mode, mode - CUT)
        squared = squared + size * size
        weight = weight * jnp.where(mode == 0, 1.0, jnp.where(mode == CUT, 0.0, 2.0))
    kinetic = squared.astype(jnp.float32) * (4.0 / CUT**2)
    kinetic = jnp.where(known & (squared < CUT * CUT), kinetic, 0.0)
    weight = weight * kinetic
    scaled, other = [], []
    for b in range(NB):
        value = spectrum[b * 24 : b * 24 + 24]
        scaled.append(value * weight)
        other.append(0.5 * kinetic * value + spectrum[(NB + b) * 24 : (NB + b) * 24 + 24])
    returned = dot(jnp.concatenate(scaled, axis=0), back[...])
    rows[...] = jnp.zeros_like(rows)
    for q, (a, b) in enumerate(PAIRS):
        term = scaled[a] * other[b] + scaled[b] * other[a]
        rows[q : q + 1, :] = jnp.sum(term[:8] + term[8:16] + term[16:], axis=0, keepdims=True)
    total = jnp.sum(rows[...], axis=1, keepdims=True) + jnp.sum(sums[...], axis=1, keepdims=True)
    picked = lax.broadcasted_iota(jnp.int32, (16, 128), 0) + 64 == lanes(16, 128)
    note = jnp.sum(jnp.where(picked, total, 0.0), axis=0, keepdims=True)
    for h in range(2):
        turned = []
        for c in range(NB * THIRDS):
            t, b = c // NB, c % NB
            value = returned[b * 24 + t * 8 : b * 24 + t * 8 + 8, h * 128 : h * 128 + 128]
            turned.append(turn(value, COLS * (c if c < 10 else c - 10)))
        for k in range(8):
            p = 8 * h + k
            value = turned[0]
            for c in range(1, 10):
                value = jnp.where(masks[k + c], turned[c], value)
            out[p * 8 : p * 8 + 8, :] = turn(value, -COLS * k)
            more[p * 8 : p * 8 + 8, :] = turn(jnp.where(masks[k + 1], turned[11], turned[10]), -COLS * k)
    pieces = [more[pl.ds(i, PENCIL, stride=8), :] for i in range(FIRSTS)]
    out[pl.ds(6, PENCIL, stride=8), :] = gathered(pieces[:5], 24, 0)
    out[pl.ds(7, PENCIL, stride=8), :] = jnp.where(lanes(PENCIL, 128) < 24, pieces[5], note)


def back_first(given, table, out):
    result = dot(table[...], jnp.concatenate([given[pl.ds(i, PENCIL, stride=8), :] for i in range(FIRSTS)], axis=0))
    for i in range(ROWS):
        out[pl.ds(i, SLAB, stride=8), :] = result[i * SLAB : (i + 1) * SLAB]
    rest = [given[pl.ds(i, PENCIL, stride=8), :] for i in (6, 7)]
    result = dot(table[...], jnp.concatenate([turn(rest[i // 5], -24 * (i % 5)) for i in range(FIRSTS)], axis=0))
    pieces = [result[i * SLAB : (i + 1) * SLAB] for i in range(ROWS)]
    out[pl.ds(6, SLAB, stride=8), :] = gathered(pieces[:5], 24, 0)
    note = jnp.sum(rest[1], axis=0, keepdims=True)
    out[pl.ds(7, SLAB, stride=8), :] = jnp.where(lanes(SLAB, 128) < 24, pieces[5], note)


def back_third(given, local, table, out, lines, low, high, sent):
    rest = [given[pl.ds(i, SLAB, stride=8), :] for i in (6, 7)]
    for i in range(ROWS):
        value = given[pl.ds(i, SLAB, stride=8), :]
        at = i * HALF
        lines[0:32, at : at + HALF] = value[:, :HALF]
        lines[32:64, at : at + HALF] = value[:, HALF:WIDE]
        lines[64:96, at : at + 24] = value[:, WIDE : WIDE + 24]
        lines[64:96, at + 24 : at + HALF] = rest[i // 5][:, 24 * (i % 5) : 24 * (i % 5) + 24]
    kinetic_part = dot(lines[...], table[...], ((0,), (0,)))
    note = jnp.sum(rest[1], axis=0, keepdims=True) * (1.0 / CELLS)
    factor, inverse = {}, {}
    for q, (a, b) in enumerate(PAIRS):
        value = note[:, 64 + q : 65 + q]
        for c in range(b):
            value = value - factor[a, c] * factor[b, c]
        if a == b:
            factor[a, a] = jnp.sqrt(value)
            inverse[a] = 1.0 / factor[a, a]
        else:
            factor[a, b] = value * inverse[b]
    copies = [pltpu.make_async_copy(low.at[i], out.at[i, :, :, 0:128], sent.at[i]) for i in range(ROWS)]
    copies += [pltpu.make_async_copy(high.at[i], out.at[i, :, :, 128:NG], sent.at[ROWS + i]) for i in range(ROWS)]
    low, high = low.reshape(ROWS * COLS * NB, 128), high.reshape(ROWS * COLS * NB, 64)
    for i in range(ROWS):
        done = []
        for a in range(NB):
            value = local[a, i] + kinetic_part[i * HALF + a * COLS : i * HALF + a * COLS + COLS]
            for b in range(a):
                value = value - factor[a, b] * done[b]
            value = value * inverse[a]
            done.append(value)
            rows = pl.ds(i * HALF + a, COLS, stride=NB)
            low[rows, :] = value[:, :128]
            high[rows, :] = value[:, 128:]
        copies[i].start()
        copies[ROWS + i].start()
    for copy in copies:
        copy.wait()


def f32(*shape):
    return jax.ShapeDtypeStruct(shape, jnp.float32)


def held(*shape):
    return pltpu.VMEM(shape, jnp.float32)


def call(body, kinds, outs, scratch=()):
    places = {"k": pltpu.VMEM, "h": pl.ANY}
    whole = [jax.tree.map(lambda _: pl.BlockSpec(memory_space=pltpu.VMEM), outs), pl.BlockSpec(memory_space=pl.ANY)]
    made = pl.pallas_call(
        body,
        out_shape=outs,
        in_specs=[pl.BlockSpec(memory_space=places[kind]) for kind in kinds],
        out_specs=whole[isinstance(outs, jax.ShapeDtypeStruct)],
        scratch_shapes=[pltpu.VMEM(shape, jnp.float32) if isinstance(shape, tuple) else shape for shape in scratch],
        name=body.__name__,
    )

    def run(*given):
        return made(*[pltpu.with_memory_space_constraint(x, places[kind]) for kind, x in zip(kinds, given)])

    return run


def trade(value, axis, number):
    blocks = value.reshape(number, -1, 8 if value.shape[0] % (8 * number) == 0 else 2, 128)
    return lax.all_to_all(blocks, axis, split_axis=0, concat_axis=0, tiled=True).reshape(value.shape)


def local_step(orbitals, potential, unlocked):
    third, first, first_back, second, second_back = tables()
    outs = (held(SLAB * 14, 128), held(NB, ROWS, COLS, NG), held(16, NG))
    scratch = [pltpu.SMEM((NB,), jnp.int32)] + [(ROWS, COLS, NB, 128), (ROWS, COLS, NB, 64), (ROWS, COLS, NG), (MODES, NG), (ROWS * WIDE, NG)]
    made = call(forward_third, "hhhh", outs, scratch + [pltpu.SemaphoreType.DMA((2 * ROWS + 3,))])
    spectrum, local, sums = made(unlocked, orbitals.transpose(1, 2, 0, 3), potential, third)
    spectrum = trade(spectrum, "slab", SLAB)
    spectrum = trade(call(forward_first, "kk", held(PENCIL * 14, 128))(spectrum, first), "pencil", PENCIL)
    scratch = [(THIRDS * 128, 128), (8 * 24, 256), (PENCIL * 8, 128), (16, 128)]
    made = call(middle, "kkkk", held(PENCIL * 8, 128), scratch)
    spectrum = trade(made(spectrum, sums, second, second_back), "pencil", PENCIL)
    spectrum = trade(call(back_first, "kk", held(SLAB * 8, 128))(spectrum, first_back), "slab", SLAB)
    scratch = [(MODES, ROWS * HALF), (ROWS, COLS, NB, 128), (ROWS, COLS, NB, 64), pltpu.SemaphoreType.DMA((2 * ROWS,))]
    made = call(back_third, "kkk", f32(ROWS, COLS, NB, NG), scratch)
    return made(spectrum, local, third).transpose(2, 0, 1, 3)


def solution(mesh):
    in_specs = (P(None, "slab", "pencil", None), P("slab", "pencil", None), P())
    out_specs = P(None, "slab", "pencil", None)
    return jax.shard_map(local_step, mesh=mesh, in_specs=in_specs, out_specs=out_specs, check_vma=False)
```

time: 81.9 us -> 80.4 us (0.982)
  blocking collectives: 75.5 us -> 74.3 us
    all_to_all x4, blocking collectives: 75.5 us -> 74.3 us  [trade(): lax.all_to_all(blocks, axis, split_axis=0, concat_axis=0, tiled=True)]
where the time goes in v6:
time: 80.4 us; the launch traced here: 80 us
  blocking collectives  74.3 us (92%)
  Pallas kernels  5.68 us (7%)
    all_to_all x4, blocking collectives, trade(): lax.all_to_all(blocks, axis, split_axis=0, concat_axis=0, tiled=True)  74.3 us
    pallas_call x5, Pallas kernels, run(): made(*[pltpu.with_memory_space_constraint(x, places[kind]) for kind, x in...  5.68 us

profile of v6, /device:TPU:1, one launch (start us, length us, event | category | flops | bytes accessed | tf_op | source)
XLA Modules:
  0.0 80.0 jit_solution(15458332973582391660)
XLA Ops:
  0.0 2.1 %forward_third.1 = (f32[448,128]{1,0:T(8,128)S(1)}, f32[4,6,12,192]{3,2,1,0:T(8,128)S(1)}, f32[16,192]{1,0:T(8,128)S(1)}) custom-call(s32[4]{0:T(128)} %flags.1, f32[6,12,4,192]{3,2,1,0:T(4,128)} %bitcast.22, f32[6,12,192]{2,1,0:T(8,128)} %potential.1, f32[96,192]{1,0:T(8,128)} %constant.10.clone.table), custom_call_target="tpu_custom_call" | custom-call | tf_op jit(solution)/shard_map/forward_third/pallas_call | solution.py:277
  2.1 0.0 copy-start.3
  2.1 18.3 %all_to_all.20 = f32[32,7,2,128]{3,2,1,0:T(2,128)S(1)} all-to-all(f32[32,7,2,128]{3,2,1,0:T(2,128)S(1)} %bitcast.21), channel_id=1, replica_groups=mesh['slab'=32,'pencil'=16] {'slab'}, dimensions={0} | all-to-all | bytes 458752 | tf_op jit(solution)/shard_map/all_to_all | solution.py:284
  20.5 0.0 copy-done.3
  20.5 0.0 copy-start.2
  20.5 0.5 forward_first.1
  20.9 0.0 copy-start.1
  20.9 25.7 %all_to_all.21 = f32[16,7,2,128]{3,2,1,0:T(2,128)S(1)} all-to-all(f32[16,7,2,128]{3,2,1,0:T(2,128)S(1)} %bitcast.18), channel_id=1, replica_groups=mesh['slab'=32,'pencil'=16] {'pencil'}, dimensions={0} | all-to-all | bytes 229376 | tf_op jit(solution)/shard_map/all_to_all | solution.py:284
  46.6 0.0 copy-done.2
  46.6 0.0 copy-done.1
  46.6 1.1 %middle.1 = f32[128,128]{1,0:T(8,128)S(1)} custom-call(f32[224,128]{1,0:T(8,128)S(1)} %bitcast.17, f32[16,192]{1,0:T(8,128)S(1)} %get-tuple-element.9.sums, f32[256,128]{1,0:T(8,128)S(1)} %copy-done.2, f32[128,256]{1,0:T(8,128)S(1)} %copy-done.1), custom_call_target="tpu_custom_call" | custom-call | tf_op jit(solution)/shard_map/middle/pallas_call | solution.py:277
  47.8 0.0 copy-start.4
  47.8 17.3 %all_to_all.22 = f32[16,1,8,128]{3,2,1,0:T(8,128)S(1)} all-to-all(f32[16,1,8,128]{3,2,1,0:T(8,128)S(1)} %bitcast.19), channel_id=1, replica_groups=mesh['slab'=32,'pencil'=16] {'pencil'}, dimensions={0} | all-to-all | bytes 131072 | tf_op jit(solution)/shard_map/all_to_all | solution.py:284
  65.1 0.0 copy-done.4
  65.1 0.4 back_first.1
  65.5 0.0 copy-start
  65.5 12.9 %all_to_all.23 = f32[32,1,8,128]{3,2,1,0:T(8,128)S(1)} all-to-all(f32[32,1,8,128]{3,2,1,0:T(8,128)S(1)} %bitcast.16), channel_id=1, replica_groups=mesh['slab'=32,'pencil'=16] {'slab'}, dimensions={0} | all-to-all | bytes 262144 | tf_op jit(solution)/shard_map/all_to_all | solution.py:284
  78.5 0.0 copy-done
  78.5 1.6 %back_third.1 = f32[6,12,4,192]{3,2,1,0:T(4,128)} custom-call(f32[256,128]{1,0:T(8,128)S(1)} %bitcast.15, f32[4,6,12,192]{3,2,1,0:T(8,128)S(1)} %get-tuple-element.10.local, f32[96,192]{1,0:T(8,128)S(1)} %copy-done), custom_call_target="tpu_custom_call" | custom-call | tf_op jit(solution)/shard_map/back_third/pallas_call | solution.py:277
Async XLA Ops:
  2.1 18.4 %copy-start.3 = (f32[96,192]{1,0:T(8,128)S(1)}, f32[96,192]{1,0:T(8,128)}, u32[]{:S(2)}) copy-start(f32[96,192]{1,0:T(8,128)} %constant.11.clone.table) | copy-start | bytes 221188
  20.5 26.2 %copy-start.2 = (f32[256,128]{1,0:T(8,128)S(1)}, f32[256,128]{1,0:T(8,128)}, u32[]{:S(2)}) copy-start(f32[256,128]{1,0:T(8,128)} %constant.12.clone.forward) | copy-start | bytes 393220
  20.9 25.7 %copy-start.1 = (f32[128,256]{1,0:T(8,128)S(1)}, f32[128,256]{1,0:T(8,128)}, u32[]{:S(2)}) copy-start(f32[128,256]{1,0:T(8,128)} %constant.13.clone.back) | copy-start | bytes 393220
  47.8 17.3 %copy-start.4 = (f32[192,96]{1,0:T(8,128)S(1)}, f32[192,96]{1,0:T(8,128)}, u32[]{:S(2)}) copy-start(f32[192,96]{1,0:T(8,128)} %constant.14.clone.table) | copy-start | bytes 221188
  65.5 13.0 %copy-start = (f32[96,192]{1,0:T(8,128)S(1)}, f32[96,192]{1,0:T(8,128)}, u32[]{:S(2)}) copy-start(f32[96,192]{1,0:T(8,128)} %constant.10.clone.table) | copy-start | bytes 221188

commit v7 on v6

--- a/solution.py
+++ b/solution.py
@@ -24,6 +24,10 @@
 PAIRS = [(a, b) for a in range(NB) for b in range(a + 1)]
 highest = lax.Precision.HIGHEST
 
+SLOTS = 16
+SPLIT = 9
+SPECIAL = 2
+
 
 def basis():
     place = np.arange(NG)
@@ -32,14 +36,53 @@
     return np.where(mode[:, None] < CUT, np.cos(angle), np.sin(angle))
 
 
+def thirds(rank):
+    return [(start + way * (rank // 2)) + CUT * (rank % 2) for start, way in ((15, -1), (16, 1), (32, 1))]
+
+
+def below(limit):
+    return [m for m in range(MODES) if m % CUT < limit and m != CUT]
+
+
+def slots():
+    kinds = [[0] * PENCIL] * 6 + [[1] * PENCIL] * 5 + [[1] * SPLIT + [2] * (PENCIL - SPLIT)] + [[2] * PENCIL] * 4
+    queues = [below(47) + [CUT, 47, 95], below(45), below(36)]
+    firsts = [[queues[kinds[slot][p]].pop(0) for p in range(PENCIL)] for slot in range(SLOTS)]
+    assert not any(queues)
+    return np.array(kinds), np.array(firsts), {PENCIL - 2: 45, PENCIL - 1: 93}
+
+
+def mode_table():
+    kinds, firsts, others = slots()
+    table = np.zeros((SLAB, PENCIL, 128))
+    weight = np.where(np.arange(MODES) == 0, 1.0, np.where(np.arange(MODES) == CUT, 0.0, 2.0))
+    for rank in range(SLAB):
+        for p in range(PENCIL):
+            for slot in range(SLOTS):
+                kind, first = kinds[slot, p], firsts[slot, p]
+                if rank < SPECIAL and slot == 5 and p in others:
+                    kind, first = 1, others[p]
+                third = thirds(rank)[kind]
+                table[rank, p, slot] = (third % CUT) ** 2 + (first % CUT) ** 2
+                table[rank, p, SLOTS + slot] = weight[third] * weight[first] / CELLS
+    return table.reshape(SLAB * PENCIL, 128)
+
+
 def tables():
     real = basis()
-    third = real.reshape(SLAB, THIRDS, NG).transpose(1, 0, 2).reshape(MODES, NG)
-    first = real.reshape(PENCIL, FIRSTS, SLAB, ROWS).transpose(1, 0, 3, 2).reshape(MODES, NG)
+    third = np.concatenate([real[[thirds(rank)[t] for rank in range(SLAB)]] for t in range(THIRDS)])
+    kinds, firsts, others = slots()
+    lines = real.reshape(MODES, SLAB, ROWS).transpose(0, 2, 1).reshape(MODES, NG)
+    rows = [np.where((kinds == t)[:, :, None], lines[firsts], 0.0) for t in range(THIRDS)]
+    extra = np.zeros((PENCIL, NG))
+    for p, m in others.items():
+        extra[p] = lines[m]
+    parts = [rows[0][0:6], np.concatenate([rows[1][6:12], extra[None]]), rows[2][11:16]]
+    parts = [part.reshape(-1, NG) for part in parts]
     second = np.zeros((128, 2, 128))
     second[:MODES, :, : NG // 2] = real.reshape(MODES, 2, NG // 2)
     second = second.reshape(128, 256)
-    made = (third, first, first.T, second.T, second)
+    made = [third, np.concatenate(parts), *[part.T for part in parts], second.T, second, mode_table()]
     return [np.ascontiguousarray(t, dtype=np.float32) for t in made]
 
 
@@ -115,36 +158,41 @@
         out[pl.ds(t * 7 + 6, SLAB, stride=14), :] = gathered(last[t * 4 : t * 4 + 4], 32, 64)
 
 
+def shared(number):
+    row = lax.broadcasted_iota(jnp.int32, (PENCIL, number), 0)
+    return (row >= PENCIL - 2) & (lax.axis_index("slab") < SPECIAL)
+
+
 def forward_first(given, table, out):
-    for t in range(2):
-        block = jnp.concatenate([given[pl.ds(t * 7 + i, SLAB, stride=14), :] for i in range(ROWS)], axis=0)
-        result = dot(table[...], block)
-        for i in range(FIRSTS):
-            out[pl.ds(t * 7 + i, PENCIL, stride=14), :] = result[i * PENCIL : (i + 1) * PENCIL]
+    blocks = [[given[pl.ds(t * 7 + i, SLAB, stride=14), :] for i in range(ROWS)] for t in range(2)]
     rest = [given[pl.ds(t * 7 + 6, SLAB, stride=14), :] for t in range(2)]
-    block = jnp.concatenate([turn(rest[i // 4], -32 * (i % 4)) for i in range(ROWS)], axis=0)
-    result = dot(table[...], block)
-    pieces = [result[i * PENCIL : (i + 1) * PENCIL] for i in range(FIRSTS)]
-    for t in range(2):
-        out[pl.ds(t * 7 + 6, PENCIL, stride=14), :] = gathered(pieces[t * 4 : t * 4 + 4], 32, 0)
-
-
-def middle(given, sums, forward, back, out, tiles, lines, more, rows):
-    rest = [given[pl.ds(t * 7 + 6, PENCIL, stride=14), :] for t in range(2)]
+    lane = lanes(SLAB, 128)
+    last = []
+    for i in range(ROWS):
+        value = jnp.where(lane < 64, turn(blocks[1][i], 64), turn(rest[i // 4], 64 - 32 * (i % 4)))
+        last.append(jnp.where(lane < 32, turn(blocks[0][i], 32), value))
+    low = dot(table[0:96, :], jnp.concatenate(blocks[0], axis=0))
+    middle = dot(table[96:208, :], jnp.concatenate(blocks[1], axis=0))
+    high = dot(table[208:288, :], jnp.concatenate(last, axis=0))
+    parts = [low[i * 16 : i * 16 + 16] for i in range(6)] + [middle[i * 16 : i * 16 + 16] for i in range(6)]
+    parts[5] = jnp.where(shared(128), middle[96:112], parts[5])
+    parts[11] = parts[11] + high[0:16]
+    parts += [high[i * 16 : i * 16 + 16] for i in range(1, 5)]
     lane = lanes(PENCIL, 128)
-    empty = jnp.zeros((PENCIL, 128), jnp.float32)
-    for i in range(8):
-        parts = [empty] * THIRDS
-        if i < FIRSTS:
-            parts = [given[pl.ds(t * 7 + i, PENCIL, stride=14), :] for t in range(2)]
-            last = jnp.where(lane < 64, turn(parts[1], 64), turn(rest[i // 4], 64 - 32 * (i % 4)))
-            parts.append(jnp.where(lane < 32, turn(parts[0], 32), last))
-        for t in range(THIRDS):
-            tiles[pl.ds(t * 128 + i, PENCIL, stride=8), :] = parts[t]
+    for i in range(12):
+        more = turn(parts[12 + i // 3], WIDE - 32 * (i % 3))
+        out[pl.ds(i, PENCIL, stride=12), :] = jnp.where(lane < WIDE, parts[i], more)
+
+
+def middle(given, sums, modes, forward, back, out, tiles, lines, rows):
+    parts = [given[pl.ds(i, PENCIL, stride=12), :] for i in range(12)]
+    parts += [gathered(parts[3 * i : 3 * i + 3], 32, WIDE) for i in range(4)]
+    for slot in range(SLOTS):
+        tiles[pl.ds(slot // 8 * 128 + slot % 8, PENCIL, stride=8), :] = parts[slot]
     lane = lanes(8, 128)
-    masks = [((lane - COLS * m) & 127) < COLS for m in range(17)]
+    masks = [((lane - COLS * m) & 127) < COLS for m in range(15)]
     for h in range(2):
-        for t in range(THIRDS):
+        for t in range(2):
             turned = []
             for k in range(8):
                 at = t * 128 + (8 * h + k) * 8
@@ -153,63 +201,63 @@
                 value = turned[0]
                 for k in range(1, 8):
                     value = jnp.where(masks[k + u], turned[k], value)
-                lines[u * 24 + t * 8 : u * 24 + t * 8 + 8, h * 128 : h * 128 + 128] = turn(value, -COLS * u)
+                at = u * SLOTS + t * 8
+                lines[at : at + 8, h * 128 : h * 128 + 128] = turn(value, -COLS * u)
     spectrum = dot(lines[...], forward[...])
-    row = lax.broadcasted_iota(jnp.int32, (24, 128), 0)
-    lane = lanes(24, 128)
-    third_mode = THIRDS * lax.axis_index("slab") + row // 8
-    first_mode = FIRSTS * lax.axis_index("pencil") + row % 8
-    known = (row % 8 < FIRSTS) & (lane < MODES)
-    squared = jnp.zeros((24, 128), jnp.int32)
-    weight = jnp.full((24, 128), 1.0 / CELLS, jnp.float32)
-    for mode in (third_mode, first_mode, lane):
-        size = jnp.where(mode < CUT, mode, mode - CUT)
-        squared = squared + size * size
-        weight = weight * jnp.where(mode == 0, 1.0, jnp.where(mode == CUT, 0.0, 2.0))
-    kinetic = squared.astype(jnp.float32) * (4.0 / CUT**2)
-    kinetic = jnp.where(known & (squared < CUT * CUT), kinetic, 0.0)
-    weight = weight * kinetic
+    lane = lanes(SLOTS, 128)
+    own = modes[pl.ds(lax.axis_index("slab") * PENCIL + lax.axis_index("pencil"), 1), :]
+    row = lax.broadcasted_iota(jnp.int32, (SLOTS, 128), 0)
+    squared = jnp.sum(jnp.where(lane == row, own, 0.0), axis=1, keepdims=True)
+    weight = jnp.sum(jnp.where(lane == row + SLOTS, own, 0.0), axis=1, keepdims=True)
+    size = jnp.where(lane < CUT, lane, lane - CUT)
+    squared = squared + (size * size).astype(jnp.float32)
+    kinetic = jnp.where((lane < MODES) & (squared < float(CUT * CUT)), squared * (4.0 / CUT**2), 0.0)
+    weight = weight * jnp.where(lane == 0, 1.0, jnp.where(lane == CUT, 0.0, 2.0)) * kinetic
     scaled, other = [], []
     for b in range(NB):
-        value = spectrum[b * 24 : b * 24 + 24]
+        value = spectrum[b * SLOTS : (b + 1) * SLOTS]
         scaled.append(value * weight)
-        other.append(0.5 * kinetic * value + spectrum[(NB + b) * 24 : (NB + b) * 24 + 24])
+        other.append(0.5 * kinetic * value + spectrum[(NB + b) * SLOTS : (NB + b + 1) * SLOTS])
     returned = dot(jnp.concatenate(scaled, axis=0), back[...])
     rows[...] = jnp.zeros_like(rows)
     for q, (a, b) in enumerate(PAIRS):
         term = scaled[a] * other[b] + scaled[b] * other[a]
-        rows[q : q + 1, :] = jnp.sum(term[:8] + term[8:16] + term[16:], axis=0, keepdims=True)
+        rows[q : q + 1, :] = jnp.sum(term, axis=0, keepdims=True)
     total = jnp.sum(rows[...], axis=1, keepdims=True) + jnp.sum(sums[...], axis=1, keepdims=True)
-    picked = lax.broadcasted_iota(jnp.int32, (16, 128), 0) + 64 == lanes(16, 128)
-    note = jnp.sum(jnp.where(picked, total, 0.0), axis=0, keepdims=True)
+    note = jnp.sum(jnp.where(lane == row + WIDE, total, 0.0), axis=0, keepdims=True)
+    lane = lanes(8, 128)
     for h in range(2):
         turned = []
-        for c in range(NB * THIRDS):
-            t, b = c // NB, c % NB
-            value = returned[b * 24 + t * 8 : b * 24 + t * 8 + 8, h * 128 : h * 128 + 128]
-            turned.append(turn(value, COLS * (c if c < 10 else c - 10)))
+        for c in range(2 * NB):
+            at = c % NB * SLOTS + c // NB * 8
+            turned.append(turn(returned[at : at + 8, h * 128 : h * 128 + 128], COLS * c))
         for k in range(8):
             p = 8 * h + k
             value = turned[0]
-            for c in range(1, 10):
+            for c in range(1, 2 * NB):
                 value = jnp.where(masks[k + c], turned[c], value)
-            out[p * 8 : p * 8 + 8, :] = turn(value, -COLS * k)
-            more[p * 8 : p * 8 + 8, :] = turn(jnp.where(masks[k + 1], turned[11], turned[10]), -COLS * k)
-    pieces = [more[pl.ds(i, PENCIL, stride=8), :] for i in range(FIRSTS)]
-    out[pl.ds(6, PENCIL, stride=8), :] = gathered(pieces[:5], 24, 0)
-    out[pl.ds(7, PENCIL, stride=8), :] = jnp.where(lanes(PENCIL, 128) < 24, pieces[5], note)
-
-
-def back_first(given, table, out):
-    result = dot(table[...], jnp.concatenate([given[pl.ds(i, PENCIL, stride=8), :] for i in range(FIRSTS)], axis=0))
-    for i in range(ROWS):
-        out[pl.ds(i, SLAB, stride=8), :] = result[i * SLAB : (i + 1) * SLAB]
-    rest = [given[pl.ds(i, PENCIL, stride=8), :] for i in (6, 7)]
-    result = dot(table[...], jnp.concatenate([turn(rest[i // 5], -24 * (i % 5)) for i in range(FIRSTS)], axis=0))
-    pieces = [result[i * SLAB : (i + 1) * SLAB] for i in range(ROWS)]
-    out[pl.ds(6, SLAB, stride=8), :] = gathered(pieces[:5], 24, 0)
-    note = jnp.sum(rest[1], axis=0, keepdims=True)
-    out[pl.ds(7, SLAB, stride=8), :] = jnp.where(lanes(SLAB, 128) < 24, pieces[5], note)
+            out[p * 8 : p * 8 + 8, :] = jnp.where(lane < WIDE, turn(value, -COLS * k), note)
+
+
+def back_first(given, low, middle, high, out):
+    parts = [given[pl.ds(i, PENCIL, stride=8), :] for i in range(8)]
+    note = jnp.sum(parts[0], axis=0, keepdims=True)
+    parts += [turn(part, -HALF) for part in parts]
+    empty = jnp.zeros((PENCIL, 128), jnp.float32)
+    here = shared(128)
+    own = [*parts[0:5], jnp.where(here, empty, parts[5])]
+    first = dot(low[...], jnp.concatenate(own, axis=0))
+    second = dot(middle[...], jnp.concatenate([*parts[6:12], jnp.where(here, parts[5], empty)], axis=0))
+    third = dot(high[...], jnp.concatenate(parts[11:16], axis=0))
+    lane = lanes(SLAB, 128)
+    pieces = []
+    for i in range(ROWS):
+        rows = slice(i * SLAB, (i + 1) * SLAB)
+        value = jnp.where(lane < WIDE, turn(second[rows], HALF), turn(third[rows], WIDE))
+        out[pl.ds(i, SLAB, stride=8), :] = jnp.where(lane < HALF, first[rows], value)
+        pieces.append(third[rows])
+    out[pl.ds(6, SLAB, stride=8), :] = gathered(pieces[:5], 24, 24)
+    out[pl.ds(7, SLAB, stride=8), :] = jnp.where(lane < 24, turn(pieces[5], -24), note)
 
 
 def back_third(given, local, table, out, lines, low, high, sent):
@@ -225,7 +273,7 @@
     note = jnp.sum(rest[1], axis=0, keepdims=True) * (1.0 / CELLS)
     factor, inverse = {}, {}
     for q, (a, b) in enumerate(PAIRS):
-        value = note[:, 64 + q : 65 + q]
+        value = note[:, WIDE + q : WIDE + q + 1]
         for c in range(b):
             value = value - factor[a, c] * factor[b, c]
         if a == b:
@@ -280,22 +328,23 @@
 
 
 def trade(value, axis, number):
-    blocks = value.reshape(number, -1, 8 if value.shape[0] % (8 * number) == 0 else 2, 128)
+    rows = next(size for size in (8, 4, 2) if value.shape[0] % (size * number) == 0)
+    blocks = value.reshape(number, -1, rows, 128)
     return lax.all_to_all(blocks, axis, split_axis=0, concat_axis=0, tiled=True).reshape(value.shape)
 
 
 def local_step(orbitals, potential, unlocked):
-    third, first, first_back, second, second_back = tables()
+    third, first, low, middle_back, high, second, second_back, modes = tables()
     outs = (held(SLAB * 14, 128), held(NB, ROWS, COLS, NG), held(16, NG))
     scratch = [pltpu.SMEM((NB,), jnp.int32)] + [(ROWS, COLS, NB, 128), (ROWS, COLS, NB, 64), (ROWS, COLS, NG), (MODES, NG), (ROWS * WIDE, NG)]
     made = call(forward_third, "hhhh", outs, scratch + [pltpu.SemaphoreType.DMA((2 * ROWS + 3,))])
     spectrum, local, sums = made(unlocked, orbitals.transpose(1, 2, 0, 3), potential, third)
     spectrum = trade(spectrum, "slab", SLAB)
-    spectrum = trade(call(forward_first, "kk", held(PENCIL * 14, 128))(spectrum, first), "pencil", PENCIL)
-    scratch = [(THIRDS * 128, 128), (8 * 24, 256), (PENCIL * 8, 128), (16, 128)]
-    made = call(middle, "kkkk", held(PENCIL * 8, 128), scratch)
-    spectrum = trade(made(spectrum, sums, second, second_back), "pencil", PENCIL)
-    spectrum = trade(call(back_first, "kk", held(SLAB * 8, 128))(spectrum, first_back), "slab", SLAB)
+    spectrum = trade(call(forward_first, "kk", held(PENCIL * 12, 128))(spectrum, first), "pencil", PENCIL)
+    made = call(middle, "kkkkk", held(PENCIL * 8, 128), [(256, 128), (2 * NB * SLOTS, 256), (16, 128)])
+    spectrum = trade(made(spectrum, sums, modes, second, second_back), "pencil", PENCIL)
+    made = call(back_first, "kkkk", held(SLAB * 8, 128))
+    spectrum = trade(made(spectrum, low, middle_back, high), "slab", SLAB)
     scratch = [(MODES, ROWS * HALF), (ROWS, COLS, NB, 128), (ROWS, COLS, NB, 64), pltpu.SemaphoreType.DMA((2 * ROWS,))]
     made = call(back_third, "kkk", f32(ROWS, COLS, NB, NG), scratch)
     return made(spectrum, local, third).transpose(2, 0, 1, 3)

time: 80.4 us -> 79.6 us (0.990)
  no operation moved by 1% of the time
where the time goes in v7:
time: 79.6 us; the launch traced here: 79.3 us
  blocking collectives  73.6 us (92%)
  Pallas kernels  5.56 us (7%)
    all_to_all x4, blocking collectives, trade(): lax.all_to_all(blocks, axis, split_axis=0, concat_axis=0, tiled=True)  73.6 us
    pallas_call x5, Pallas kernels, run(): made(*[pltpu.with_memory_space_constraint(x, places[kind]) for kind, x in...  5.56 us

profile of v7, /device:TPU:1, one launch (start us, length us, event | category | flops | bytes accessed | tf_op | source)
XLA Modules:
  0.0 79.3 jit_solution(17807705019813518773)
XLA Ops:
  0.0 2.1 %forward_third.1 = (f32[448,128]{1,0:T(8,128)S(1)}, f32[4,6,12,192]{3,2,1,0:T(8,128)S(1)}, f32[16,192]{1,0:T(8,128)S(1)}) custom-call(s32[4]{0:T(128)} %flags.1, f32[6,12,4,192]{3,2,1,0:T(4,128)} %bitcast.22, f32[6,12,192]{2,1,0:T(8,128)} %potential.1, f32[96,192]{1,0:T(8,128)} %constant.16.clone.table), custom_call_target="tpu_custom_call" | custom-call | tf_op jit(solution)/shard_map/forward_third/pallas_call | solution.py:325
  2.1 0.0 copy-start.1
  2.1 18.3 %all_to_all.20 = f32[32,7,2,128]{3,2,1,0:T(2,128)S(1)} all-to-all(f32[32,7,2,128]{3,2,1,0:T(2,128)S(1)} %bitcast.21), channel_id=1, replica_groups=mesh['slab'=32,'pencil'=16] {'slab'}, dimensions={0} | all-to-all | bytes 458752 | tf_op jit(solution)/shard_map/all_to_all | solution.py:333
  20.5 0.0 copy-done.1
  20.5 0.0 copy-start.2
  20.5 0.0 copy-start.4
  20.5 0.5 forward_first.1
  21.0 0.0 copy-start.3
  21.0 25.6 %all_to_all.21 = f32[16,3,4,128]{3,2,1,0:T(4,128)S(1)} all-to-all(f32[16,3,4,128]{3,2,1,0:T(4,128)S(1)} %bitcast.17), channel_id=1, replica_groups=mesh['slab'=32,'pencil'=16] {'pencil'}, dimensions={0} | all-to-all | bytes 196608 | tf_op jit(solution)/shard_map/all_to_all | solution.py:333
  46.6 0.0 copy-done.2
  46.6 0.0 copy-done.4
  46.6 0.0 copy-done.3
  46.6 0.0 copy-start.6
  46.6 0.0 copy-start.7
  46.6 0.9 %middle.2 = f32[128,128]{1,0:T(8,128)S(1)} custom-call(f32[192,128]{1,0:T(8,128)S(1)} %bitcast.18, f32[16,192]{1,0:T(8,128)S(1)} %get-tuple-element.9.sums, f32[512,128]{1,0:T(8,128)S(1)} %copy-done.2, f32[256,128]{1,0:T(8,128)S(1)} %copy-done.4, f32[128,256]{1,0:T(8,128)S(1)} %copy-done.3), custom_call_target="tpu_custom_call" | custom-call | tf_op jit(solution)/shard_map/middle/pallas_call | solution.py:325
  47.5 0.0 copy-start.5
  47.5 16.6 %all_to_all.22 = f32[16,1,8,128]{3,2,1,0:T(8,128)S(1)} all-to-all(f32[16,1,8,128]{3,2,1,0:T(8,128)S(1)} %bitcast.20), channel_id=1, replica_groups=mesh['slab'=32,'pencil'=16] {'pencil'}, dimensions={0} | all-to-all | bytes 131072 | tf_op jit(solution)/shard_map/all_to_all | solution.py:333
  64.1 0.0 copy-done.6
  64.1 0.0 copy-done.7
  64.1 0.0 copy-done.5
  64.1 0.5 back_first.1
  64.6 0.0 copy-start
  64.7 13.1 %all_to_all.23 = f32[32,1,8,128]{3,2,1,0:T(8,128)S(1)} all-to-all(f32[32,1,8,128]{3,2,1,0:T(8,128)S(1)} %bitcast.16), channel_id=1, replica_groups=mesh['slab'=32,'pencil'=16] {'slab'}, dimensions={0} | all-to-all | bytes 262144 | tf_op jit(solution)/shard_map/all_to_all | solution.py:333
  77.7 0.0 copy-done
  77.7 1.6 %back_third.1 = f32[6,12,4,192]{3,2,1,0:T(4,128)} custom-call(f32[256,128]{1,0:T(8,128)S(1)} %bitcast.15, f32[4,6,12,192]{3,2,1,0:T(8,128)S(1)} %get-tuple-element.10.local, f32[96,192]{1,0:T(8,128)S(1)} %copy-done), custom_call_target="tpu_custom_call" | custom-call | tf_op jit(solution)/shard_map/back_third/pallas_call | solution.py:325
Async XLA Ops:
  2.1 18.4 %copy-start.1 = (f32[288,192]{1,0:T(8,128)S(1)}, f32[288,192]{1,0:T(8,128)}, u32[]{:S(2)}) copy-start(f32[288,192]{1,0:T(8,128)} %constant.17.clone.table) | copy-start | bytes 663556
  20.5 26.1 %copy-start.2 = (f32[512,128]{1,0:T(8,128)S(1)}, f32[512,128]{1,0:T(8,128)}, u32[]{:S(2)}) copy-start(f32[512,128]{1,0:T(8,128)} %constant.18.clone.modes) | copy-start | bytes 786436
  20.5 26.1 %copy-start.4 = (f32[256,128]{1,0:T(8,128)S(1)}, f32[256,128]{1,0:T(8,128)}, u32[]{:S(2)}) copy-start(f32[256,128]{1,0:T(8,128)} %constant.19.clone.forward) | copy-start | bytes 393220
  21.0 25.6 %copy-start.3 = (f32[128,256]{1,0:T(8,128)S(1)}, f32[128,256]{1,0:T(8,128)}, u32[]{:S(2)}) copy-start(f32[128,256]{1,0:T(8,128)} %constant.20.clone.back) | copy-start | bytes 393220
  46.6 17.5 %copy-start.6 = (f32[192,112]{1,0:T(8,128)S(1)}, f32[192,112]{1,0:T(8,128)}, u32[]{:S(2)}) copy-start(f32[192,112]{1,0:T(8,128)} %constant.22.clone.middle) | copy-start | bytes 258052
  46.6 17.5 %copy-start.7 = (f32[192,96]{1,0:T(8,128)S(1)}, f32[192,96]{1,0:T(8,128)}, u32[]{:S(2)}) copy-start(f32[192,96]{1,0:T(8,128)} %constant.21.clone.low) | copy-start | bytes 221188
  47.5 16.6 %copy-start.5 = (f32[192,80]{1,0:T(8,128)S(1)}, f32[192,80]{1,0:T(8,128)}, u32[]{:S(2)}) copy-start(f32[192,80]{1,0:T(8,128)} %constant.23.clone.high) | copy-start | bytes 184324
  64.6 13.1 %copy-start = (f32[96,192]{1,0:T(8,128)S(1)}, f32[96,192]{1,0:T(8,128)}, u32[]{:S(2)}) copy-start(f32[96,192]{1,0:T(8,128)} %constant.16.clone.table) | copy-start | bytes 221188

commit v8 on v7

--- a/solution.py
+++ b/solution.py
@@ -82,7 +82,12 @@
     second = np.zeros((128, 2, 128))
     second[:MODES, :, : NG // 2] = real.reshape(MODES, 2, NG // 2)
     second = second.reshape(128, 256)
-    made = [third, np.concatenate(parts), *[part.T for part in parts], second.T, second, mode_table()]
+    every = lines[firsts]
+    back = every.reshape(-1, NG).T.copy()
+    for p, m in others.items():
+        every[5, p] = lines[m]
+    special = every.reshape(-1, NG).T[:, 0:128]
+    made = [third, np.concatenate(parts), back, special, second.T, second, mode_table()]
     return [np.ascontiguousarray(t, dtype=np.float32) for t in made]
 
 
@@ -129,7 +134,7 @@
             parts = [ref[pl.ds(i * WIDE // 2 + b, COLS, stride=NB), :] for ref in (low, high)]
             value = jnp.concatenate([parts[0], parts[1]], axis=1)
             kept = jnp.where(kind[b] == 1, value * shifted, value)
-            lines[base : base + COLS, :] = value * jnp.where(kind[b] == 1, 1.0 / 1.5, 0.0)
+            lines[base : base + COLS, :] = value
             lines[base + HALF : base + HALF + COLS, :] = kept
             local[b, i] = kept
             own.append(kept)
@@ -139,6 +144,11 @@
     copies[-1].wait()
     whole = lanes(SLAB, 128)
     last = []
+    lane = lanes(MODES, 128)
+    scale = jnp.ones((MODES, 128), jnp.float32)
+    for b in range(NB):
+        alpha = jnp.where(kind[b] == 1, 1.0 / 1.5, 0.0)
+        scale = jnp.where((lane >= b * COLS) & (lane < (b + 1) * COLS), alpha, scale)
     for i in range(ROWS):
         if i % 2 == 0:
             spectrum = dot(made[...], lines[i * WIDE : i * WIDE + 2 * WIDE, :], ((1,), (1,)))
@@ -146,6 +156,7 @@
         else:
             more = jnp.concatenate([spectrum[:, 128:], jnp.zeros((MODES, 64), jnp.float32)], axis=1)
             result = jnp.where(lanes(MODES, 128) < 32, turn(spectrum[:, :128], 32), turn(more, 32))
+        result = result * scale
         parts = [result[t * 32 : t * 32 + 32] for t in range(THIRDS)]
         for t in range(2):
             extra = turn(parts[2], WIDE - 32 * t)
@@ -225,7 +236,6 @@
         rows[q : q + 1, :] = jnp.sum(term, axis=0, keepdims=True)
     total = jnp.sum(rows[...], axis=1, keepdims=True) + jnp.sum(sums[...], axis=1, keepdims=True)
     note = jnp.sum(jnp.where(lane == row + WIDE, total, 0.0), axis=0, keepdims=True)
-    lane = lanes(8, 128)
     for h in range(2):
         turned = []
         for c in range(2 * NB):
@@ -236,41 +246,63 @@
             value = turned[0]
             for c in range(1, 2 * NB):
                 value = jnp.where(masks[k + c], turned[c], value)
-            out[p * 8 : p * 8 + 8, :] = jnp.where(lane < WIDE, turn(value, -COLS * k), note)
-
-
-def back_first(given, low, middle, high, out):
-    parts = [given[pl.ds(i, PENCIL, stride=8), :] for i in range(8)]
-    note = jnp.sum(parts[0], axis=0, keepdims=True)
-    parts += [turn(part, -HALF) for part in parts]
+            tiles[p * 8 : p * 8 + 8, :] = turn(value, -COLS * k)
+    parts = [tiles[pl.ds(i, PENCIL, stride=8), :] for i in range(8)]
+    lane = lanes(PENCIL, 128)
+    for i in range(6):
+        more = turn(parts[6 + i // 3], WIDE - 32 * (i % 3))
+        out[pl.ds(i, PENCIL, stride=7), :] = jnp.where(lane < WIDE, parts[i], more)
+    out[pl.ds(6, PENCIL, stride=7), :] = jnp.broadcast_to(note, (PENCIL, 128))
+
+
+def back_first(given, table, special, out):
+    parts = [given[pl.ds(i, PENCIL, stride=7), :] for i in range(6)]
+    note = jnp.sum(given[pl.ds(6, PENCIL, stride=7), :], axis=0, keepdims=True)
+    parts += [gathered(parts[3 * i : 3 * i + 3], 32, WIDE) for i in range(2)]
+    parts += parts
+    lane = lanes(PENCIL, 128)
+    row = lax.broadcasted_iota(jnp.int32, (PENCIL, 128), 0)
+    inside = [lane < HALF, (lane >= HALF) & (lane < WIDE), lane >= WIDE, lane < 16]
+    main, more = [], []
     empty = jnp.zeros((PENCIL, 128), jnp.float32)
-    here = shared(128)
-    own = [*parts[0:5], jnp.where(here, empty, parts[5])]
-    first = dot(low[...], jnp.concatenate(own, axis=0))
-    second = dot(middle[...], jnp.concatenate([*parts[6:12], jnp.where(here, parts[5], empty)], axis=0))
-    third = dot(high[...], jnp.concatenate(parts[11:16], axis=0))
-    lane = lanes(SLAB, 128)
+    for slot in range(SLOTS):
+        moved = turn(parts[slot], HALF)
+        if slot < 6:
+            value = jnp.where(inside[0], parts[slot], 0.0)
+            if slot == 5:
+                value = jnp.where(shared(128), jnp.where(inside[1], moved, 0.0), value)
+        else:
+            value = jnp.where(inside[1], moved if slot < 8 else parts[slot], 0.0)
+        rest = empty
+        if slot > 10:
+            late = jnp.where(inside[2], moved, 0.0)
+            rest = jnp.where(inside[3], moved, 0.0)
+            if slot == 11:
+                late, rest = jnp.where(row < SPLIT, value, late), jnp.where(row < SPLIT, 0.0, rest)
+            value = late
+        main.append(value)
+        more.append(rest)
+    given_all = jnp.concatenate([jnp.concatenate(main, axis=0), jnp.concatenate(more, axis=0)], axis=1)
+    first = jnp.where(lax.axis_index("slab") < SPECIAL, special[...], table[:, 0:128])
+    result = dot(jnp.concatenate([first, table[:, 128:256]], axis=1), given_all)
     pieces = []
     for i in range(ROWS):
-        rows = slice(i * SLAB, (i + 1) * SLAB)
-        value = jnp.where(lane < WIDE, turn(second[rows], HALF), turn(third[rows], WIDE))
-        out[pl.ds(i, SLAB, stride=8), :] = jnp.where(lane < HALF, first[rows], value)
-        pieces.append(third[rows])
-    out[pl.ds(6, SLAB, stride=8), :] = gathered(pieces[:5], 24, 24)
-    out[pl.ds(7, SLAB, stride=8), :] = jnp.where(lane < 24, turn(pieces[5], -24), note)
-
-
-def back_third(given, local, table, out, lines, low, high, sent):
-    rest = [given[pl.ds(i, SLAB, stride=8), :] for i in (6, 7)]
-    for i in range(ROWS):
-        value = given[pl.ds(i, SLAB, stride=8), :]
+        out[pl.ds(i, SLAB, stride=7), :] = result[i * SLAB : (i + 1) * SLAB, 0:128]
+        pieces.append(result[i * SLAB : (i + 1) * SLAB, 128:256])
+    out[pl.ds(6, SLAB, stride=7), :] = jnp.where(lanes(SLAB, 128) < WIDE, gathered(pieces, 16, 0), note)
+
+
+def back_third(given, local, table, out, lines):
+    rest = given[pl.ds(6, SLAB, stride=7), :]
+    for i in range(ROWS):
+        value = given[pl.ds(i, SLAB, stride=7), :]
         at = i * HALF
         lines[0:32, at : at + HALF] = value[:, :HALF]
         lines[32:64, at : at + HALF] = value[:, HALF:WIDE]
-        lines[64:96, at : at + 24] = value[:, WIDE : WIDE + 24]
-        lines[64:96, at + 24 : at + HALF] = rest[i // 5][:, 24 * (i % 5) : 24 * (i % 5) + 24]
+        lines[64:96, at : at + 32] = value[:, WIDE:128]
+        lines[64:96, at + 32 : at + HALF] = rest[:, 16 * i : 16 * i + 16]
     kinetic_part = dot(lines[...], table[...], ((0,), (0,)))
-    note = jnp.sum(rest[1], axis=0, keepdims=True) * (1.0 / CELLS)
+    note = jnp.sum(rest, axis=0, keepdims=True) * (1.0 / CELLS)
     factor, inverse = {}, {}
     for q, (a, b) in enumerate(PAIRS):
         value = note[:, WIDE + q : WIDE + q + 1]
@@ -281,9 +313,6 @@
             inverse[a] = 1.0 / factor[a, a]
         else:
             factor[a, b] = value * inverse[b]
-    copies = [pltpu.make_async_copy(low.at[i], out.at[i, :, :, 0:128], sent.at[i]) for i in range(ROWS)]
-    copies += [pltpu.make_async_copy(high.at[i], out.at[i, :, :, 128:NG], sent.at[ROWS + i]) for i in range(ROWS)]
-    low, high = low.reshape(ROWS * COLS * NB, 128), high.reshape(ROWS * COLS * NB, 64)
     for i in range(ROWS):
         done = []
         for a in range(NB):
@@ -292,13 +321,7 @@
                 value = value - factor[a, b] * done[b]
             value = value * inverse[a]
             done.append(value)
-            rows = pl.ds(i * HALF + a, COLS, stride=NB)
-            low[rows, :] = value[:, :128]
-            high[rows, :] = value[:, 128:]
-        copies[i].start()
-        copies[ROWS + i].start()
-    for copy in copies:
-        copy.wait()
+            out[i, :, a, :] = value
 
 
 def f32(*shape):
@@ -311,12 +334,11 @@
 
 def call(body, kinds, outs, scratch=()):
     places = {"k": pltpu.VMEM, "h": pl.ANY}
-    whole = [jax.tree.map(lambda _: pl.BlockSpec(memory_space=pltpu.VMEM), outs), pl.BlockSpec(memory_space=pl.ANY)]
     made = pl.pallas_call(
         body,
         out_shape=outs,
         in_specs=[pl.BlockSpec(memory_space=places[kind]) for kind in kinds],
-        out_specs=whole[isinstance(outs, jax.ShapeDtypeStruct)],
+        out_specs=jax.tree.map(lambda _: pl.BlockSpec(memory_space=pltpu.VMEM), outs),
         scratch_shapes=[pltpu.VMEM(shape, jnp.float32) if isinstance(shape, tuple) else shape for shape in scratch],
         name=body.__name__,
     )
@@ -328,25 +350,24 @@
 
 
 def trade(value, axis, number):
-    rows = next(size for size in (8, 4, 2) if value.shape[0] % (size * number) == 0)
+    rows = next(size for size in (8, 4, 2, 1) if value.shape[0] % (size * number) == 0)
     blocks = value.reshape(number, -1, rows, 128)
     return lax.all_to_all(blocks, axis, split_axis=0, concat_axis=0, tiled=True).reshape(value.shape)
 
 
 def local_step(orbitals, potential, unlocked):
-    third, first, low, middle_back, high, second, second_back, modes = tables()
+    third, first, first_back, special, second, second_back, modes = tables()
     outs = (held(SLAB * 14, 128), held(NB, ROWS, COLS, NG), held(16, NG))
     scratch = [pltpu.SMEM((NB,), jnp.int32)] + [(ROWS, COLS, NB, 128), (ROWS, COLS, NB, 64), (ROWS, COLS, NG), (MODES, NG), (ROWS * WIDE, NG)]
     made = call(forward_third, "hhhh", outs, scratch + [pltpu.SemaphoreType.DMA((2 * ROWS + 3,))])
     spectrum, local, sums = made(unlocked, orbitals.transpose(1, 2, 0, 3), potential, third)
     spectrum = trade(spectrum, "slab", SLAB)
     spectrum = trade(call(forward_first, "kk", held(PENCIL * 12, 128))(spectrum, first), "pencil", PENCIL)
-    made = call(middle, "kkkkk", held(PENCIL * 8, 128), [(256, 128), (2 * NB * SLOTS, 256), (16, 128)])
+    made = call(middle, "kkkkk", held(PENCIL * 7, 128), [(256, 128), (2 * NB * SLOTS, 256), (16, 128)])
     spectrum = trade(made(spectrum, sums, modes, second, second_back), "pencil", PENCIL)
-    made = call(back_first, "kkkk", held(SLAB * 8, 128))
-    spectrum = trade(made(spectrum, low, middle_back, high), "slab", SLAB)
-    scratch = [(MODES, ROWS * HALF), (ROWS, COLS, NB, 128), (ROWS, COLS, NB, 64), pltpu.SemaphoreType.DMA((2 * ROWS,))]
-    made = call(back_third, "kkk", f32(ROWS, COLS, NB, NG), scratch)
+    made = call(back_first, "kkk", held(SLAB * 7, 128))
+    spectrum = trade(made(spectrum, first_back, special), "slab", SLAB)
+    made = call(back_third, "kkk", f32(ROWS, COLS, NB, NG), [(MODES, ROWS * HALF)])
     return made(spectrum, local, third).transpose(2, 0, 1, 3)
 
 

time: 79.6 us -> 79.5 us (level)
  no operation moved by 1% of the time
where the time goes in v8:
time: 79.5 us; the launch traced here: 79.2 us
  blocking collectives  73.4 us (92%)
  Pallas kernels  5.61 us (7%)
    all_to_all x4, blocking collectives, trade(): lax.all_to_all(blocks, axis, split_axis=0, concat_axis=0, tiled=True)  73.4 us
    pallas_call x5, Pallas kernels, run(): made(*[pltpu.with_memory_space_constraint(x, places[kind]) for kind, x in...  5.61 us

profile of v8, /device:TPU:1, one launch (start us, length us, event | category | flops | bytes accessed | tf_op | source)
XLA Modules:
  0.0 79.2 jit_solution(1006324187103973026)
XLA Ops:
  0.0 2.1 %forward_third.1 = (f32[448,128]{1,0:T(8,128)S(1)}, f32[4,6,12,192]{3,2,1,0:T(8,128)S(1)}, f32[16,192]{1,0:T(8,128)S(1)}) custom-call(s32[4]{0:T(128)} %flags.1, f32[6,12,4,192]{3,2,1,0:T(4,128)} %bitcast.18, f32[6,12,192]{2,1,0:T(8,128)} %potential.1, f32[96,192]{1,0:T(8,128)} %constant.14.clone.table), custom_call_target="tpu_custom_call" | custom-call | tf_op jit(solution)/shard_map/forward_third/pallas_call | solution.py:347
  2.1 0.0 copy-start.1
  2.1 18.3 %all_to_all.20 = f32[32,7,2,128]{3,2,1,0:T(2,128)S(1)} all-to-all(f32[32,7,2,128]{3,2,1,0:T(2,128)S(1)} %bitcast.16), channel_id=1, replica_groups=mesh['slab'=32,'pencil'=16] {'slab'}, dimensions={0} | all-to-all | bytes 458752 | tf_op jit(solution)/shard_map/all_to_all | solution.py:355
  20.5 0.0 copy-done.1
  20.5 0.0 copy-start.2
  20.5 0.0 copy-start.5
  20.5 0.5 forward_first.1
  21.0 0.0 copy-start.4
  21.0 25.6 %all_to_all.21 = f32[16,3,4,128]{3,2,1,0:T(4,128)S(1)} all-to-all(f32[16,3,4,128]{3,2,1,0:T(4,128)S(1)} %bitcast.13), channel_id=1, replica_groups=mesh['slab'=32,'pencil'=16] {'pencil'}, dimensions={0} | all-to-all | bytes 196608 | tf_op jit(solution)/shard_map/all_to_all | solution.py:355
  46.6 0.0 copy-done.2
  46.6 0.0 copy-done.5
  46.6 0.0 copy-done.4
  46.6 0.0 copy-start.3
  46.6 1.0 %middle.1 = f32[112,128]{1,0:T(8,128)S(1)} custom-call(f32[192,128]{1,0:T(8,128)S(1)} %bitcast.14, f32[16,192]{1,0:T(8,128)S(1)} %get-tuple-element.9.sums, f32[512,128]{1,0:T(8,128)S(1)} %copy-done.2, f32[256,128]{1,0:T(8,128)S(1)} %copy-done.5, f32[128,256]{1,0:T(8,128)S(1)} %copy-done.4), custom_call_target="tpu_custom_call" | custom-call | tf_op jit(solution)/shard_map/middle/pallas_call | solution.py:347
  47.6 0.0 copy-start.6
  47.6 16.7 %all_to_all.22 = f32[16,7,1,128]{3,2,1,0:T(1,128)S(1)} all-to-all(f32[16,7,1,128]{3,2,1,0:T(1,128)S(1)} %bitcast.17), channel_id=1, replica_groups=mesh['slab'=32,'pencil'=16] {'pencil'}, dimensions={0} | all-to-all | bytes 114688 | tf_op jit(solution)/shard_map/all_to_all | solution.py:355
  64.3 0.0 copy-done.3
  64.3 0.0 copy-done.6
  64.3 0.5 back_first.1
  64.8 0.0 copy-start
  64.8 12.8 %all_to_all.23 = f32[32,7,1,128]{3,2,1,0:T(1,128)S(1)} all-to-all(f32[32,7,1,128]{3,2,1,0:T(1,128)S(1)} %bitcast.12), channel_id=1, replica_groups=mesh['slab'=32,'pencil'=16] {'slab'}, dimensions={0} | all-to-all | bytes 229376 | tf_op jit(solution)/shard_map/all_to_all | solution.py:355
  77.6 0.0 copy-done
  77.6 1.5 %back_third.1 = f32[6,12,4,192]{3,2,1,0:T(4,128)} custom-call(f32[224,128]{1,0:T(8,128)S(1)} %bitcast.11, f32[4,6,12,192]{3,2,1,0:T(8,128)S(1)} %get-tuple-element.10.local, f32[96,192]{1,0:T(8,128)S(1)} %copy-done), custom_call_target="tpu_custom_call" | custom-call | tf_op jit(solution)/shard_map/back_third/pallas_call | solution.py:347
Async XLA Ops:
  2.1 18.4 %copy-start.1 = (f32[288,192]{1,0:T(8,128)S(1)}, f32[288,192]{1,0:T(8,128)}, u32[]{:S(2)}) copy-start(f32[288,192]{1,0:T(8,128)} %constant.15.clone.table) | copy-start | bytes 663556
  20.5 26.1 %copy-start.2 = (f32[512,128]{1,0:T(8,128)S(1)}, f32[512,128]{1,0:T(8,128)}, u32[]{:S(2)}) copy-start(f32[512,128]{1,0:T(8,128)} %constant.16.clone.modes) | copy-start | bytes 786436
  20.5 26.1 %copy-start.5 = (f32[256,128]{1,0:T(8,128)S(1)}, f32[256,128]{1,0:T(8,128)}, u32[]{:S(2)}) copy-start(f32[256,128]{1,0:T(8,128)} %constant.17.clone.forward) | copy-start | bytes 393220
  21.0 25.6 %copy-start.4 = (f32[128,256]{1,0:T(8,128)S(1)}, f32[128,256]{1,0:T(8,128)}, u32[]{:S(2)}) copy-start(f32[128,256]{1,0:T(8,128)} %constant.18.clone.back) | copy-start | bytes 393220
  46.6 17.7 %copy-start.3 = (f32[192,256]{1,0:T(8,128)S(1)}, f32[192,256]{1,0:T(8,128)}, u32[]{:S(2)}) copy-start(f32[192,256]{1,0:T(8,128)} %constant.19.clone.table) | copy-start | bytes 589828
  47.6 16.7 %copy-start.6 = (f32[192,128]{1,0:T(8,128)S(1)}, f32[192,128]{1,0:T(8,128)}, u32[]{:S(2)}) copy-start(f32[192,128]{1,0:T(8,128)} %constant.20.clone.special) | copy-start | bytes 294916
  64.8 12.9 %copy-start = (f32[96,192]{1,0:T(8,128)S(1)}, f32[96,192]{1,0:T(8,128)}, u32[]{:S(2)}) copy-start(f32[96,192]{1,0:T(8,128)} %constant.14.clone.table) | copy-start | bytes 221188

commit v9 on v8

--- a/solution.py
+++ b/solution.py
@@ -65,7 +65,7 @@
                 third = thirds(rank)[kind]
                 table[rank, p, slot] = (third % CUT) ** 2 + (first % CUT) ** 2
                 table[rank, p, SLOTS + slot] = weight[third] * weight[first] / CELLS
-    return table.reshape(SLAB * PENCIL, 128)
+    return np.concatenate([table.reshape(SLAB * PENCIL, 128), np.zeros((8, 128))])
 
 
 def tables():
@@ -115,18 +115,19 @@
 
 def forward_third(flags, orbitals, potential, table, out, local, sums, kind, low, high, field, made, lines, ready):
     copies = [pltpu.make_async_copy(flags, kind, ready.at[0]), pltpu.make_async_copy(potential, field, ready.at[1])]
-    copies += [pltpu.make_async_copy(orbitals.at[i, :, :, 0:128], low.at[i], ready.at[2 + i]) for i in range(ROWS)]
-    copies += [pltpu.make_async_copy(orbitals.at[i, :, :, 128:NG], high.at[i], ready.at[2 + ROWS + i]) for i in range(ROWS)]
+    for i in range(ROWS):
+        copies.append(pltpu.make_async_copy(orbitals.at[i, :, :, 0:128], low.at[i], ready.at[2 + 2 * i]))
+        copies.append(pltpu.make_async_copy(orbitals.at[i, :, :, 128:NG], high.at[i], ready.at[3 + 2 * i]))
     copies.append(pltpu.make_async_copy(table, made, ready.at[2 + 2 * ROWS]))
-    low, high = low.reshape(ROWS * COLS * NB, 128), high.reshape(ROWS * COLS * NB, 64)
+    low, high = low.reshape((ROWS + 1) * COLS * NB, 128), high.reshape((ROWS + 1) * COLS * NB, 64)
     for copy in copies:
         copy.start()
     copies[0].wait()
     copies[1].wait()
     totals = [None] * len(PAIRS)
     for i in range(ROWS):
-        copies[2 + i].wait()
-        copies[2 + ROWS + i].wait()
+        copies[2 + 2 * i].wait()
+        copies[3 + 2 * i].wait()
         shifted = (field[i] - 1.0) * (1.0 / 1.5)
         own = []
         for b in range(NB):
@@ -358,7 +359,7 @@
 def local_step(orbitals, potential, unlocked):
     third, first, first_back, special, second, second_back, modes = tables()
     outs = (held(SLAB * 14, 128), held(NB, ROWS, COLS, NG), held(16, NG))
-    scratch = [pltpu.SMEM((NB,), jnp.int32)] + [(ROWS, COLS, NB, 128), (ROWS, COLS, NB, 64), (ROWS, COLS, NG), (MODES, NG), (ROWS * WIDE, NG)]
+    scratch = [pltpu.SMEM((NB,), jnp.int32)] + [(ROWS + 1, COLS, NB, 128), (ROWS + 1, COLS, NB, 64), (ROWS, COLS, NG), (MODES, NG), (ROWS * WIDE, NG)]
     made = call(forward_third, "hhhh", outs, scratch + [pltpu.SemaphoreType.DMA((2 * ROWS + 3,))])
     spectrum, local, sums = made(unlocked, orbitals.transpose(1, 2, 0, 3), potential, third)
     spectrum = trade(spectrum, "slab", SLAB)

time: 79.5 us -> 79.5 us (level)
  no operation moved by 1% of the time
where the time goes in v9:
time: 79.5 us; the launch traced here: 79.2 us
  blocking collectives  73.4 us (92%)
  Pallas kernels  5.6 us (7%)
    all_to_all x4, blocking collectives, trade(): lax.all_to_all(blocks, axis, split_axis=0, concat_axis=0, tiled=True)  73.4 us
    pallas_call x5, Pallas kernels, run(): made(*[pltpu.with_memory_space_constraint(x, places[kind]) for kind, x in...  5.6 us

profile of v9, /device:TPU:1, one launch (start us, length us, event | category | flops | bytes accessed | tf_op | source)
XLA Modules:
  0.0 79.2 jit_solution(2991618433522231914)
XLA Ops:
  0.0 2.1 %forward_third.1 = (f32[448,128]{1,0:T(8,128)S(1)}, f32[4,6,12,192]{3,2,1,0:T(8,128)S(1)}, f32[16,192]{1,0:T(8,128)S(1)}) custom-call(s32[4]{0:T(128)} %flags.1, f32[6,12,4,192]{3,2,1,0:T(4,128)} %bitcast.18, f32[6,12,192]{2,1,0:T(8,128)} %potential.1, f32[96,192]{1,0:T(8,128)} %constant.14.clone.table), custom_call_target="tpu_custom_call" | custom-call | tf_op jit(solution)/shard_map/forward_third/pallas_call | solution.py:348
  2.1 0.0 copy-start.1
  2.1 18.3 %all_to_all.20 = f32[32,7,2,128]{3,2,1,0:T(2,128)S(1)} all-to-all(f32[32,7,2,128]{3,2,1,0:T(2,128)S(1)} %bitcast.16), channel_id=1, replica_groups=mesh['slab'=32,'pencil'=16] {'slab'}, dimensions={0} | all-to-all | bytes 458752 | tf_op jit(solution)/shard_map/all_to_all | solution.py:356
  20.5 0.0 copy-done.1
  20.5 0.0 copy-start.2
  20.5 0.0 copy-start.5
  20.5 0.5 forward_first.1
  21.0 0.0 copy-start.4
  21.0 25.6 %all_to_all.21 = f32[16,3,4,128]{3,2,1,0:T(4,128)S(1)} all-to-all(f32[16,3,4,128]{3,2,1,0:T(4,128)S(1)} %bitcast.13), channel_id=1, replica_groups=mesh['slab'=32,'pencil'=16] {'pencil'}, dimensions={0} | all-to-all | bytes 196608 | tf_op jit(solution)/shard_map/all_to_all | solution.py:356
  46.6 0.0 copy-done.2
  46.6 0.0 copy-done.5
  46.6 0.0 copy-done.4
  46.6 0.0 copy-start.3
  46.6 1.0 %middle.1 = f32[112,128]{1,0:T(8,128)S(1)} custom-call(f32[192,128]{1,0:T(8,128)S(1)} %bitcast.14, f32[16,192]{1,0:T(8,128)S(1)} %get-tuple-element.9.sums, f32[520,128]{1,0:T(8,128)S(1)} %copy-done.2, f32[256,128]{1,0:T(8,128)S(1)} %copy-done.5, f32[128,256]{1,0:T(8,128)S(1)} %copy-done.4), custom_call_target="tpu_custom_call" | custom-call | tf_op jit(solution)/shard_map/middle/pallas_call | solution.py:348
  47.6 0.0 copy-start.6
  47.6 16.7 %all_to_all.22 = f32[16,7,1,128]{3,2,1,0:T(1,128)S(1)} all-to-all(f32[16,7,1,128]{3,2,1,0:T(1,128)S(1)} %bitcast.17), channel_id=1, replica_groups=mesh['slab'=32,'pencil'=16] {'pencil'}, dimensions={0} | all-to-all | bytes 114688 | tf_op jit(solution)/shard_map/all_to_all | solution.py:356
  64.3 0.0 copy-done.3
  64.3 0.0 copy-done.6
  64.3 0.5 back_first.1
  64.8 0.0 copy-start
  64.8 12.8 %all_to_all.23 = f32[32,7,1,128]{3,2,1,0:T(1,128)S(1)} all-to-all(f32[32,7,1,128]{3,2,1,0:T(1,128)S(1)} %bitcast.12), channel_id=1, replica_groups=mesh['slab'=32,'pencil'=16] {'slab'}, dimensions={0} | all-to-all | bytes 229376 | tf_op jit(solution)/shard_map/all_to_all | solution.py:356
  77.6 0.0 copy-done
  77.6 1.5 %back_third.1 = f32[6,12,4,192]{3,2,1,0:T(4,128)} custom-call(f32[224,128]{1,0:T(8,128)S(1)} %bitcast.11, f32[4,6,12,192]{3,2,1,0:T(8,128)S(1)} %get-tuple-element.10.local, f32[96,192]{1,0:T(8,128)S(1)} %copy-done), custom_call_target="tpu_custom_call" | custom-call | tf_op jit(solution)/shard_map/back_third/pallas_call | solution.py:348
Async XLA Ops:
  2.1 18.4 %copy-start.1 = (f32[288,192]{1,0:T(8,128)S(1)}, f32[288,192]{1,0:T(8,128)}, u32[]{:S(2)}) copy-start(f32[288,192]{1,0:T(8,128)} %constant.15.clone.table) | copy-start | bytes 663556
  20.5 26.1 %copy-start.2 = (f32[520,128]{1,0:T(8,128)S(1)}, f32[520,128]{1,0:T(8,128)}, u32[]{:S(2)}) copy-start(f32[520,128]{1,0:T(8,128)} %constant.16.clone.modes) | copy-start | bytes 798724
  20.5 26.1 %copy-start.5 = (f32[256,128]{1,0:T(8,128)S(1)}, f32[256,128]{1,0:T(8,128)}, u32[]{:S(2)}) copy-start(f32[256,128]{1,0:T(8,128)} %constant.17.clone.forward) | copy-start | bytes 393220
  21.0 25.6 %copy-start.4 = (f32[128,256]{1,0:T(8,128)S(1)}, f32[128,256]{1,0:T(8,128)}, u32[]{:S(2)}) copy-start(f32[128,256]{1,0:T(8,128)} %constant.18.clone.back) | copy-start | bytes 393220
  46.6 17.7 %copy-start.3 = (f32[192,256]{1,0:T(8,128)S(1)}, f32[192,256]{1,0:T(8,128)}, u32[]{:S(2)}) copy-start(f32[192,256]{1,0:T(8,128)} %constant.19.clone.table) | copy-start | bytes 589828
  47.6 16.7 %copy-start.6 = (f32[192,128]{1,0:T(8,128)S(1)}, f32[192,128]{1,0:T(8,128)}, u32[]{:S(2)}) copy-start(f32[192,128]{1,0:T(8,128)} %constant.20.clone.special) | copy-start | bytes 294916
  64.8 12.9 %copy-start = (f32[96,192]{1,0:T(8,128)S(1)}, f32[96,192]{1,0:T(8,128)}, u32[]{:S(2)}) copy-start(f32[96,192]{1,0:T(8,128)} %constant.14.clone.table) | copy-start | bytes 221188

commit v10 on v9

--- a/solution.py
+++ b/solution.py
@@ -351,7 +351,7 @@
 
 
 def trade(value, axis, number):
-    rows = next(size for size in (8, 4, 2, 1) if value.shape[0] % (size * number) == 0)
+    rows = next(size for size in (1,) if value.shape[0] % (size * number) == 0)
     blocks = value.reshape(number, -1, rows, 128)
     return lax.all_to_all(blocks, axis, split_axis=0, concat_axis=0, tiled=True).reshape(value.shape)
 

time: 79.5 us -> 79.5 us (level)
  no operation moved by 1% of the time
where the time goes in v10:
time: 79.5 us; the launch traced here: 79.2 us
  blocking collectives  73.4 us (92%)
  Pallas kernels  5.6 us (7%)
    all_to_all x4, blocking collectives, trade(): lax.all_to_all(blocks, axis, split_axis=0, concat_axis=0, tiled=True)  73.4 us
    pallas_call x5, Pallas kernels, run(): made(*[pltpu.with_memory_space_constraint(x, places[kind]) for kind, x in...  5.6 us

profile of v10, /device:TPU:1, one launch (start us, length us, event | category | flops | bytes accessed | tf_op | source)
XLA Modules:
  0.0 79.2 jit_solution(2991618433522231914)
XLA Ops:
  0.0 2.1 %forward_third.1 = (f32[448,128]{1,0:T(8,128)S(1)}, f32[4,6,12,192]{3,2,1,0:T(8,128)S(1)}, f32[16,192]{1,0:T(8,128)S(1)}) custom-call(s32[4]{0:T(128)} %flags.1, f32[6,12,4,192]{3,2,1,0:T(4,128)} %bitcast.18, f32[6,12,192]{2,1,0:T(8,128)} %potential.1, f32[96,192]{1,0:T(8,128)} %constant.14.clone.table), custom_call_target="tpu_custom_call" | custom-call | tf_op jit(solution)/shard_map/forward_third/pallas_call | solution.py:348
  2.1 0.0 copy-start.1
  2.1 18.3 %all_to_all.20 = f32[32,14,1,128]{3,2,1,0:T(1,128)S(1)} all-to-all(f32[32,14,1,128]{3,2,1,0:T(1,128)S(1)} %bitcast.16), channel_id=1, replica_groups=mesh['slab'=32,'pencil'=16] {'slab'}, dimensions={0} | all-to-all | bytes 458752 | tf_op jit(solution)/shard_map/all_to_all | solution.py:356
  20.5 0.0 copy-done.1
  20.5 0.0 copy-start.2
  20.5 0.0 copy-start.5
  20.5 0.5 forward_first.1
  21.0 0.0 copy-start.4
  21.0 25.6 %all_to_all.21 = f32[16,12,1,128]{3,2,1,0:T(1,128)S(1)} all-to-all(f32[16,12,1,128]{3,2,1,0:T(1,128)S(1)} %bitcast.13), channel_id=1, replica_groups=mesh['slab'=32,'pencil'=16] {'pencil'}, dimensions={0} | all-to-all | bytes 196608 | tf_op jit(solution)/shard_map/all_to_all | solution.py:356
  46.6 0.0 copy-done.2
  46.6 0.0 copy-done.5
  46.6 0.0 copy-done.4
  46.6 0.0 copy-start.3
  46.6 1.0 %middle.1 = f32[112,128]{1,0:T(8,128)S(1)} custom-call(f32[192,128]{1,0:T(8,128)S(1)} %bitcast.14, f32[16,192]{1,0:T(8,128)S(1)} %get-tuple-element.9.sums, f32[520,128]{1,0:T(8,128)S(1)} %copy-done.2, f32[256,128]{1,0:T(8,128)S(1)} %copy-done.5, f32[128,256]{1,0:T(8,128)S(1)} %copy-done.4), custom_call_target="tpu_custom_call" | custom-call | tf_op jit(solution)/shard_map/middle/pallas_call | solution.py:348
  47.6 0.0 copy-start.6
  47.6 16.7 %all_to_all.22 = f32[16,7,1,128]{3,2,1,0:T(1,128)S(1)} all-to-all(f32[16,7,1,128]{3,2,1,0:T(1,128)S(1)} %bitcast.17), channel_id=1, replica_groups=mesh['slab'=32,'pencil'=16] {'pencil'}, dimensions={0} | all-to-all | bytes 114688 | tf_op jit(solution)/shard_map/all_to_all | solution.py:356
  64.3 0.0 copy-done.3
  64.3 0.0 copy-done.6
  64.3 0.5 back_first.1
  64.8 0.0 copy-start
  64.8 12.8 %all_to_all.23 = f32[32,7,1,128]{3,2,1,0:T(1,128)S(1)} all-to-all(f32[32,7,1,128]{3,2,1,0:T(1,128)S(1)} %bitcast.12), channel_id=1, replica_groups=mesh['slab'=32,'pencil'=16] {'slab'}, dimensions={0} | all-to-all | bytes 229376 | tf_op jit(solution)/shard_map/all_to_all | solution.py:356
  77.6 0.0 copy-done
  77.6 1.5 %back_third.1 = f32[6,12,4,192]{3,2,1,0:T(4,128)} custom-call(f32[224,128]{1,0:T(8,128)S(1)} %bitcast.11, f32[4,6,12,192]{3,2,1,0:T(8,128)S(1)} %get-tuple-element.10.local, f32[96,192]{1,0:T(8,128)S(1)} %copy-done), custom_call_target="tpu_custom_call" | custom-call | tf_op jit(solution)/shard_map/back_third/pallas_call | solution.py:348
Async XLA Ops:
  2.1 18.4 %copy-start.1 = (f32[288,192]{1,0:T(8,128)S(1)}, f32[288,192]{1,0:T(8,128)}, u32[]{:S(2)}) copy-start(f32[288,192]{1,0:T(8,128)} %constant.15.clone.table) | copy-start | bytes 663556
  20.5 26.1 %copy-start.2 = (f32[520,128]{1,0:T(8,128)S(1)}, f32[520,128]{1,0:T(8,128)}, u32[]{:S(2)}) copy-start(f32[520,128]{1,0:T(8,128)} %constant.16.clone.modes) | copy-start | bytes 798724
  20.5 26.1 %copy-start.5 = (f32[256,128]{1,0:T(8,128)S(1)}, f32[256,128]{1,0:T(8,128)}, u32[]{:S(2)}) copy-start(f32[256,128]{1,0:T(8,128)} %constant.17.clone.forward) | copy-start | bytes 393220
  21.0 25.6 %copy-start.4 = (f32[128,256]{1,0:T(8,128)S(1)}, f32[128,256]{1,0:T(8,128)}, u32[]{:S(2)}) copy-start(f32[128,256]{1,0:T(8,128)} %constant.18.clone.back) | copy-start | bytes 393220
  46.6 17.7 %copy-start.3 = (f32[192,256]{1,0:T(8,128)S(1)}, f32[192,256]{1,0:T(8,128)}, u32[]{:S(2)}) copy-start(f32[192,256]{1,0:T(8,128)} %constant.19.clone.table) | copy-start | bytes 589828
  47.6 16.7 %copy-start.6 = (f32[192,128]{1,0:T(8,128)S(1)}, f32[192,128]{1,0:T(8,128)}, u32[]{:S(2)}) copy-start(f32[192,128]{1,0:T(8,128)} %constant.20.clone.special) | copy-start | bytes 294916
  64.8 12.9 %copy-start = (f32[96,192]{1,0:T(8,128)S(1)}, f32[96,192]{1,0:T(8,128)}, u32[]{:S(2)}) copy-start(f32[96,192]{1,0:T(8,128)} %constant.14.clone.table) | copy-start | bytes 221188

commit v11 on v9

--- a/solution.py
+++ b/solution.py
@@ -115,9 +115,9 @@
 
 def forward_third(flags, orbitals, potential, table, out, local, sums, kind, low, high, field, made, lines, ready):
     copies = [pltpu.make_async_copy(flags, kind, ready.at[0]), pltpu.make_async_copy(potential, field, ready.at[1])]
-    for i in range(ROWS):
-        copies.append(pltpu.make_async_copy(orbitals.at[i, :, :, 0:128], low.at[i], ready.at[2 + 2 * i]))
-        copies.append(pltpu.make_async_copy(orbitals.at[i, :, :, 128:NG], high.at[i], ready.at[3 + 2 * i]))
+    for i in range(0, ROWS, 2):
+        copies.append(pltpu.make_async_copy(orbitals.at[i : i + 2, :, :, 0:128], low.at[i : i + 2], ready.at[2 + 2 * i]))
+        copies.append(pltpu.make_async_copy(orbitals.at[i : i + 2, :, :, 128:NG], high.at[i : i + 2], ready.at[3 + 2 * i]))
     copies.append(pltpu.make_async_copy(table, made, ready.at[2 + 2 * ROWS]))
     low, high = low.reshape((ROWS + 1) * COLS * NB, 128), high.reshape((ROWS + 1) * COLS * NB, 64)
     for copy in copies:
@@ -126,8 +126,9 @@
     copies[1].wait()
     totals = [None] * len(PAIRS)
     for i in range(ROWS):
-        copies[2 + 2 * i].wait()
-        copies[3 + 2 * i].wait()
+        if i % 2 == 0:
+            copies[2 + i // 2 * 2].wait()
+            copies[3 + i // 2 * 2].wait()
         shifted = (field[i] - 1.0) * (1.0 / 1.5)
         own = []
         for b in range(NB):

time: 79.5 us -> 79.5 us (level)
  no operation moved by 1% of the time
where the time goes in v11:
time: 79.5 us; the launch traced here: 79.1 us
  blocking collectives  73.4 us (92%)
  Pallas kernels  5.59 us (7%)
    all_to_all x4, blocking collectives, trade(): lax.all_to_all(blocks, axis, split_axis=0, concat_axis=0, tiled=True)  73.4 us
    pallas_call x5, Pallas kernels, run(): made(*[pltpu.with_memory_space_constraint(x, places[kind]) for kind, x in...  5.59 us

profile of v11, /device:TPU:1, one launch (start us, length us, event | category | flops | bytes accessed | tf_op | source)
XLA Modules:
  0.0 79.1 jit_solution(3763220641386574119)
XLA Ops:
  0.0 2.1 %forward_third.1 = (f32[448,128]{1,0:T(8,128)S(1)}, f32[4,6,12,192]{3,2,1,0:T(8,128)S(1)}, f32[16,192]{1,0:T(8,128)S(1)}) custom-call(s32[4]{0:T(128)} %flags.1, f32[6,12,4,192]{3,2,1,0:T(4,128)} %bitcast.18, f32[6,12,192]{2,1,0:T(8,128)} %potential.1, f32[96,192]{1,0:T(8,128)} %constant.14.clone.table), custom_call_target="tpu_custom_call" | custom-call | tf_op jit(solution)/shard_map/forward_third/pallas_call | solution.py:349
  2.1 0.0 copy-start.1
  2.1 18.3 %all_to_all.20 = f32[32,7,2,128]{3,2,1,0:T(2,128)S(1)} all-to-all(f32[32,7,2,128]{3,2,1,0:T(2,128)S(1)} %bitcast.16), channel_id=1, replica_groups=mesh['slab'=32,'pencil'=16] {'slab'}, dimensions={0} | all-to-all | bytes 458752 | tf_op jit(solution)/shard_map/all_to_all | solution.py:357
  20.5 0.0 copy-done.1
  20.5 0.0 copy-start.2
  20.5 0.0 copy-start.5
  20.5 0.5 forward_first.1
  21.0 0.0 copy-start.4
  21.0 25.6 %all_to_all.21 = f32[16,3,4,128]{3,2,1,0:T(4,128)S(1)} all-to-all(f32[16,3,4,128]{3,2,1,0:T(4,128)S(1)} %bitcast.13), channel_id=1, replica_groups=mesh['slab'=32,'pencil'=16] {'pencil'}, dimensions={0} | all-to-all | bytes 196608 | tf_op jit(solution)/shard_map/all_to_all | solution.py:357
  46.6 0.0 copy-done.2
  46.6 0.0 copy-done.5
  46.6 0.0 copy-done.4
  46.6 0.0 copy-start.3
  46.6 1.0 %middle.1 = f32[112,128]{1,0:T(8,128)S(1)} custom-call(f32[192,128]{1,0:T(8,128)S(1)} %bitcast.14, f32[16,192]{1,0:T(8,128)S(1)} %get-tuple-element.9.sums, f32[520,128]{1,0:T(8,128)S(1)} %copy-done.2, f32[256,128]{1,0:T(8,128)S(1)} %copy-done.5, f32[128,256]{1,0:T(8,128)S(1)} %copy-done.4), custom_call_target="tpu_custom_call" | custom-call | tf_op jit(solution)/shard_map/middle/pallas_call | solution.py:349
  47.5 0.0 copy-start.6
  47.6 16.7 %all_to_all.22 = f32[16,7,1,128]{3,2,1,0:T(1,128)S(1)} all-to-all(f32[16,7,1,128]{3,2,1,0:T(1,128)S(1)} %bitcast.17), channel_id=1, replica_groups=mesh['slab'=32,'pencil'=16] {'pencil'}, dimensions={0} | all-to-all | bytes 114688 | tf_op jit(solution)/shard_map/all_to_all | solution.py:357
  64.2 0.0 copy-done.3
  64.2 0.0 copy-done.6
  64.2 0.5 back_first.1
  64.8 0.0 copy-start
  64.8 12.8 %all_to_all.23 = f32[32,7,1,128]{3,2,1,0:T(1,128)S(1)} all-to-all(f32[32,7,1,128]{3,2,1,0:T(1,128)S(1)} %bitcast.12), channel_id=1, replica_groups=mesh['slab'=32,'pencil'=16] {'slab'}, dimensions={0} | all-to-all | bytes 229376 | tf_op jit(solution)/shard_map/all_to_all | solution.py:357
  77.6 0.0 copy-done
  77.6 1.5 %back_third.1 = f32[6,12,4,192]{3,2,1,0:T(4,128)} custom-call(f32[224,128]{1,0:T(8,128)S(1)} %bitcast.11, f32[4,6,12,192]{3,2,1,0:T(8,128)S(1)} %get-tuple-element.10.local, f32[96,192]{1,0:T(8,128)S(1)} %copy-done), custom_call_target="tpu_custom_call" | custom-call | tf_op jit(solution)/shard_map/back_third/pallas_call | solution.py:349
Async XLA Ops:
  2.1 18.4 %copy-start.1 = (f32[288,192]{1,0:T(8,128)S(1)}, f32[288,192]{1,0:T(8,128)}, u32[]{:S(2)}) copy-start(f32[288,192]{1,0:T(8,128)} %constant.15.clone.table) | copy-start | bytes 663556
  20.5 26.1 %copy-start.2 = (f32[520,128]{1,0:T(8,128)S(1)}, f32[520,128]{1,0:T(8,128)}, u32[]{:S(2)}) copy-start(f32[520,128]{1,0:T(8,128)} %constant.16.clone.modes) | copy-start | bytes 798724
  20.5 26.1 %copy-start.5 = (f32[256,128]{1,0:T(8,128)S(1)}, f32[256,128]{1,0:T(8,128)}, u32[]{:S(2)}) copy-start(f32[256,128]{1,0:T(8,128)} %constant.17.clone.forward) | copy-start | bytes 393220
  21.0 25.6 %copy-start.4 = (f32[128,256]{1,0:T(8,128)S(1)}, f32[128,256]{1,0:T(8,128)}, u32[]{:S(2)}) copy-start(f32[128,256]{1,0:T(8,128)} %constant.18.clone.back) | copy-start | bytes 393220
  46.6 17.7 %copy-start.3 = (f32[192,256]{1,0:T(8,128)S(1)}, f32[192,256]{1,0:T(8,128)}, u32[]{:S(2)}) copy-start(f32[192,256]{1,0:T(8,128)} %constant.19.clone.table) | copy-start | bytes 589828
  47.5 16.7 %copy-start.6 = (f32[192,128]{1,0:T(8,128)S(1)}, f32[192,128]{1,0:T(8,128)}, u32[]{:S(2)}) copy-start(f32[192,128]{1,0:T(8,128)} %constant.20.clone.special) | copy-start | bytes 294916
  64.8 12.9 %copy-start = (f32[96,192]{1,0:T(8,128)S(1)}, f32[96,192]{1,0:T(8,128)}, u32[]{:S(2)}) copy-start(f32[96,192]{1,0:T(8,128)} %constant.14.clone.table) | copy-start | bytes 221188
